TPU v7x, 32 devices: a whole 2x2x4 slice. The times are simulated.
32 devices in a mesh: grp: 2 (over x), box: 16 (over z, y, core).
Axes of the slice: x: 2, y: 2, z: 4, core: 2. Of those that a mesh axis runs over, the one named last changes fastest.
Arguments:
- coarse_state: float32 [5, 128, 64, 128], P(None, 'box', 'grp'), parts along dimension 2, may hold values from -1 to 5.75, as said below
- fine_state: float32 [256, 5, 16, 256], P(('grp', 'box')), parts along dimension 0, may hold values from -1 to 5.75, as said below
- patch_box: int32 [256], P('grp'), parts along dimension 0, may hold values from 0 to 1023, as said below
- face_flags: int32 [256, 6], P('grp'), parts along dimension 0, may hold values from 0 to 1, as said below
Outputs:
- coarse_next: float32 [5, 128, 64, 128], P(None, 'box', 'grp'), parts along dimension 2
- fine_next: float32 [256, 5, 16, 256], P(('grp', 'box')), parts along dimension 0
There are 2 independent parts, one for each index of `grp`. A program takes and returns all parts, laid end to end along the dimension named above; each array names one. Nothing has to cross between parts.
Inputs may be any that keep to these rules, and one draw needn't show every extreme that they name: `patch_box`: all entries are distinct coarse boxes. Of the 8 patches held by one device (aligned blocks of rows), at most 1 lie on boxes of one index of box, and that many do in every block. `face_flags`: A flag is 1 exactly when the coarse box across that face (periodic) is refined by no patch. `coarse_state`: density lies in 0.5 to 2, velocities in -0.5 to 0.5 and pressure in 0.5 to 2 in every cell. `fine_state`: density lies in 0.5 to 2, velocities in -0.5 to 0.5 and pressure in 0.5 to 2 in every cell.
All inputs are finite; a program needn't handle non-finite values.
Results may differ from a plain program's by a relative error of at most 0.0003.
Values sent between devices are 32-bit elements; how exact they have to be, the bound alone decides.
No kernel may reach another device: no remote copies, remote signals or barrier semaphores. Data moves between devices by JAX's collectives and lax.ppermute only.
A program may use at most 256 MiB of HBM per device.

v0:
```python
import functools

import jax
import jax.numpy as jnp
from jax import lax
from jax.experimental import pallas as pl
from jax.experimental.pallas import tpu as pltpu
from jax.sharding import PartitionSpec as P

gas_gamma = 1.4
time_step = 0.05

NF = 5
CW = 8
FW = 16
NP = 8
LN = 128
ZC = 32
YB = LN // CW
SIDE = ((0, 0), (0, 33), (0, 66), (1, 0), (1, 33))
XUNIT = tuple((0, 99 + 8 * u) if u < 3 else (1, 66 + 8 * (u - 3)) for u in range(10))


def take_lanes(values, index):
    return jnp.take_along_axis(values, index, axis=1, mode="promise_in_bounds")


def lanes():
    return lax.broadcasted_iota(jnp.int32, (8, LN), 1)


def roll_to(values, shift):
    if isinstance(shift, int):
        shift = shift % LN
        return values if shift == 0 else pltpu.roll(values, shift, 1)
    return pltpu.roll(values, shift & (LN - 1), 1)


def primitives(state):
    inverse = 1.0 / state[0]
    speeds = [None] + [state[m] * inverse for m in (1, 2, 3)]
    squares = state[1] * speeds[1] + state[2] * speeds[2] + state[3] * speeds[3]
    pressure = (gas_gamma - 1.0) * (state[4] - 0.5 * squares)
    sound = jnp.sqrt(gas_gamma * pressure * inverse)
    return speeds, pressure, sound, state[4] + pressure


def side_of_face(state, prims, m):
    speeds, pressure, sound, total = prims
    v = speeds[m]
    flux = [state[m], state[1] * v, state[2] * v, state[3] * v, total * v]
    flux[m] = flux[m] + pressure
    return list(state) + flux + [jnp.abs(v) + sound]


def face_flux(left, right):
    fastest = jnp.maximum(left[10], right[10])
    return [left[5 + f] + right[5 + f] - fastest * (right[f] - left[f]) for f in range(NF)]


def split_box(number, per_device):
    if per_device & (per_device - 1) == 0:
        return number >> (per_device.bit_length() - 1), number & (per_device - 1)
    owner = lax.div(number, jnp.int32(per_device))
    return owner, number - owner * per_device


def find_slots(box_ref, source, me, count, per_device):
    after = jnp.where(me == count - 1, 0, me + 1)
    before = jnp.where(me == 0, count - 1, me - 1)
    found = [jnp.int32(-1)] * 3
    rows = [jnp.int32(0)] * 3
    for j in range(NP):
        row = source * NP + j
        owner, place = split_box(box_ref[row], per_device)
        for which, slab in enumerate((me, after, before)):
            hit = owner == slab
            found[which] = jnp.where(hit, place, found[which])
            rows[which] = jnp.where(hit, row, rows[which])
    return found, rows


def anchors(place):
    return (place >> 4) * CW, (place & (YB - 1)) * CW


def pack_kernel(count, box_ref, coarse_ref, out_ref, first_ref, last_ref):
    me = lax.axis_index("box")
    per_device = ZC // CW * YB
    lane = lanes()
    for f in range(NF):
        first_ref[pl.ds(f * ZC, ZC), :] = coarse_ref[pl.ds(f * 256, ZC), :]
        last_ref[pl.ds(f * ZC, ZC), :] = coarse_ref[pl.ds(f * 256 + 7 * ZC, ZC), :]

    def one(source, carry):
        (own, after, before), _ = find_slots(box_ref, source, me, count, per_device)
        tiles = [jnp.zeros((8, LN), jnp.float32)] * 2
        for u in range(10):
            f, upper = u // 2, u % 2
            place = jnp.maximum(before if upper else after, 0)
            z0, y0 = anchors(place)
            plane = 0 if upper else CW - 1
            values = coarse_ref[pl.ds(pl.multiple_of(f * 256 + plane * ZC + z0, 8), 8), :]
            tile, base = XUNIT[u]
            moved = roll_to(values, base - y0)
            tiles[tile] = jnp.where((lane >= base) & (lane < base + 8), moved, tiles[tile])
        row0 = pl.multiple_of(source * 16, 16)
        out_ref[pl.ds(row0, 8), :] = tiles[0]
        out_ref[pl.ds(row0 + 8, 8), :] = tiles[1]

        @pl.when(own >= 0)
        def _():
            z0, y0 = anchors(own)
            below = (z0 - 1) & (ZC - 1)
            above = (z0 + CW) & (ZC - 1)
            sides = [jnp.zeros((8, LN), jnp.float32)] * 2
            for f in range(NF):
                low = coarse_ref[pl.ds(f * 256 + below, 8, stride=ZC), :]
                high = coarse_ref[pl.ds(f * 256 + above, 8, stride=ZC), :]
                piece = jnp.where(lane < 8, roll_to(low, -y0), roll_to(high, 8 - y0))
                for k in range(CW):
                    values = coarse_ref[pl.ds(f * 256 + z0 + k, 8, stride=ZC), :]
                    moved = roll_to(values, 17 + k - y0)
                    piece = jnp.where((lane == 16 + k) | (lane == 25 + k), moved, piece)
                tile, base = SIDE[f]
                piece = roll_to(piece, base)
                sides[tile] = jnp.where((lane >= base) & (lane < base + 33), piece, sides[tile])
            out_ref[pl.ds(row0, 8), :] = jnp.where(lane < 99, sides[0], out_ref[pl.ds(row0, 8), :])
            out_ref[pl.ds(row0 + 8, 8), :] = jnp.where(lane < 66, sides[1], out_ref[pl.ds(row0 + 8, 8), :])

        return carry

    lax.fori_loop(0, count, one, 0)


def fine_kernel(
    count,
    box_ref,
    ghost_ref,
    fine_ref,
    next_ref,
    out_ref,
    message,
    zghost,
    yghost,
    xghost,
    state,
    carry,
    zsum,
    ysum,
    xsum,
    packed,
    given,
    semaphores,
):
    per_device = ZC // CW * YB
    me = lax.axis_index("box")
    lane = lanes()
    halves = [pl.ds(c * LN, LN) for c in range(2)]
    loads = [pltpu.make_async_copy(fine_ref.at[:, halves[c]], given.at[c], semaphores.at[c]) for c in range(2)]
    for copy in loads:
        copy.start()
    place_y = lane & 15
    first_y = place_y == 0
    last_y = place_y == 15
    low16 = lane < 16
    high16 = lane < 112

    def slots(p):
        owner, _ = split_box(box_ref[me * NP + p], per_device)
        return owner, jnp.where(owner == 0, count - 1, owner - 1), jnp.where(owner == count - 1, 0, owner + 1)

    for p in range(NP):
        own, before, after = slots(p)
        for tile in range(2):
            start = 99 if tile == 0 else 66
            lower_parity = 0 if tile == 0 else 1
            is_x = lane >= start
            is_lower = (((lane - start) >> 3) & 1) == lower_parity
            pieces = [ghost_ref[pl.ds(pl.multiple_of(s * 16 + tile * 8, 8), 8), :] for s in (own, before, after)]
            message[pl.ds(p * 16 + tile * 8, 8), :] = jnp.where(
                is_x, jnp.where(is_lower, pieces[1], pieces[2]), pieces[0]
            )
    pair_y = place_y >> 1
    for r in range(CW):
        rows = [message[pl.ds(tile * 8 + r, 8, stride=16), :] for tile in range(2)]
        along_z = []
        along_y = [[], []]
        for f in range(NF):
            tile, base = SIDE[f]
            along_z.append(take_lanes(rows[tile], jnp.where(lane < 64, base, base + 8) + pair_y))
            for c in range(2):
                index = jnp.where(place_y < 8, base + 16, base + 25) + (lane >> 5) + 4 * c
                along_y[c].append(take_lanes(rows[tile], index))
        for i, v in enumerate(side_of_face(along_z, primitives(along_z), 3)):
            zghost[i, r] = v
        for c in range(2):
            for i, v in enumerate(side_of_face(along_y[c], primitives(along_y[c]), 2)):
                yghost[i, r, c] = v
        for u in range(10):
            tile, base = XUNIT[u]
            moved = take_lanes(rows[tile], base + pair_y)
            f, upper = u // 2, u % 2
            c = r // 4
            if r % 4 == 0:
                xghost[upper, f, c] = moved
            else:
                xghost[upper, f, c] = jnp.where((lane >> 5) == r % 4, moved, xghost[upper, f, c])
    for upper in range(2):
        for c in range(2):
            values = [xghost[upper, f, c] for f in range(NF)]
            for i, v in enumerate(side_of_face(values, primitives(values), 1)):
                xghost[upper, i, c] = v

    step = 0.5 * time_step

    def substep(first):
        def finish(plane, part, flux):
            for c in range(2):
                for f in range(NF):
                    value = part[c][f] - step * flux[c][f]
                    state[f, plane, c] = value

        for c in range(2):
            for i in range(11):
                carry[i, c] = xghost[0, i, c]
            for f in range(NF):
                carry[11 + f, c] = jnp.zeros((8, LN), jnp.float32)

        def pair(r, unused):
            zg = [zghost[i, r] for i in range(11)]
            zb = [None] * NF
            yb = [[None] * NF for _ in range(2)]
            for half in range(2):
                x = 2 * r + half
                if first:
                    cells = [
                        [given[c, pl.ds(f * FW + x, NP, stride=NF * FW), :] for f in range(NF)] for c in range(2)
                    ]
                else:
                    cells = [[state[f, x + 1, c] for f in range(NF)] for c in range(2)]
                prims = [primitives(u) for u in cells]
                flux_x = []
                for c in range(2):
                    here = side_of_face(cells[c], prims[c], 1)
                    behind = [carry[i, c] for i in range(11)]
                    flux_x.append(face_flux(behind, here))
                    for i in range(11):
                        carry[i, c] = here[i]
                finish(x, [[carry[11 + f, c] for f in range(NF)] for c in range(2)], flux_x)

                if half == 0:

                    @pl.when(r == 0)
                    def _():
                        for c in range(2):
                            for f in range(NF):
                                value = flux_x[c][f]
                                xsum[0, f, c] = value if first else xsum[0, f, c] + value

                here = [side_of_face(cells[c], prims[c], 3) for c in range(2)]
                turned = [[roll_to(v, 16) for v in here[c]] for c in range(2)]
                left = [
                    [jnp.where(low16, zg[i], turned[0][i]) for i in range(11)],
                    [jnp.where(low16, turned[0][i], turned[1][i]) for i in range(11)],
                ]
                lower = [face_flux(left[c], here[c]) for c in range(2)]
                last = face_flux(here[1], zg)
                change = [[], []]
                for f in range(NF):
                    back = [roll_to(lower[c][f], -16) for c in range(2)]
                    change[0].append(jnp.where(high16, back[0], back[1]) - lower[0][f])
                    change[1].append(jnp.where(high16, back[1], last[f]) - lower[1][f])
                    edge = jnp.where(lane < 64, lower[0][f], last[f])
                    zb[f] = edge if half == 0 else zb[f] + edge
                for c in range(2):
                    yg = [yghost[i, r, c] for i in range(11)]
                    here = side_of_face(cells[c], prims[c], 2)
                    left = [jnp.where(first_y, yg[i], roll_to(here[i], 1)) for i in range(11)]
                    lower_y = face_flux(left, here)
                    last_flux = face_flux(here, yg)
                    for f in range(NF):
                        upper_y = jnp.where(last_y, last_flux[f], roll_to(lower_y[f], -1))
                        change[c][f] = change[c][f] + (upper_y - lower_y[f])
                        edge = jnp.where(place_y < 8, lower_y[f], last_flux[f])
                        yb[c][f] = edge if half == 0 else yb[c][f] + edge
                for c in range(2):
                    for f in range(NF):
                        carry[11 + f, c] = cells[c][f] - step * (change[c][f] - flux_x[c][f])
            for f in range(NF):
                zsum[f, r] = zb[f] if first else zsum[f, r] + zb[f]
                for c in range(2):
                    ysum[f, r, c] = yb[c][f] if first else ysum[f, r, c] + yb[c][f]
            return unused

        lax.fori_loop(0, CW, pair, 0)
        flux_x = [
            face_flux([carry[i, c] for i in range(11)], [xghost[1, i, c] for i in range(11)]) for c in range(2)
        ]
        finish(FW, [[carry[11 + f, c] for f in range(NF)] for c in range(2)], flux_x)
        for c in range(2):
            for f in range(NF):
                value = flux_x[c][f]
                xsum[1, f, c] = value if first else xsum[1, f, c] + value

    for copy in loads:
        copy.wait()
    substep(True)
    substep(False)

    source_avg = ((lane & 31) >> 3) * 32 + (lane & 7) * 2
    source_z = jnp.where(lane < 88, (lane - 80) * 2, 112 + (lane - 88) * 2) & (LN - 1)
    source_y = jnp.where(lane < 72, 0, 15) + (lane & 3) * 32
    for f in range(NF):
        xpool = []
        for side in range(2):
            cols = []
            for c in range(2):
                v = xsum[side, f, c]
                v = v + roll_to(v, -1)
                cols.append(v + roll_to(v, -16))
            xpool.append(cols)

        for r in range(CW):
            average = None
            for c in range(2):
                v = []
                for half in range(2):
                    value = state[f, 2 * r + half + 1, c]
                    given[c, pl.ds(f * FW + 2 * r + half, NP, stride=NF * FW), :] = value
                    v.append(value)
                v = v[0] + v[1]
                v = v + roll_to(v, -1)
                v = v + roll_to(v, -16)
                v = take_lanes(v, source_avg)
                average = v if c == 0 else jnp.where(lane < 32, average, v)
            v = zsum[f, r]
            z_part = take_lanes(v + roll_to(v, -1), source_z)
            y_part = []
            for c in range(2):
                v = ysum[f, r, c]
                y_part.append(take_lanes(v + roll_to(v, -16), source_y))
            y_part = jnp.where((lane & 7) < 4, y_part[0], y_part[1])
            source_x = (r % 4) * 32 + (lane & 7) * 2
            x_part = [take_lanes(xpool[side][r // 4], source_x) for side in range(2)]
            x_part = jnp.where(lane < 104, x_part[0], x_part[1])
            fluxes = jnp.where(lane < 80, y_part, jnp.where(lane < 96, z_part, x_part)) * 0.0625
            row = jnp.where(lane < 64, average * 0.125, fluxes)
            packed[pl.ds(f * 8 + r, NP, stride=NF * 8), :] = row

    stores = [pltpu.make_async_copy(given.at[c], next_ref.at[:, halves[c]], semaphores.at[2 + c]) for c in range(2)]
    for copy in stores:
        copy.start()
    for p in range(NP):
        own, before, after = slots(p)
        for f in range(NF):
            tile = packed[pl.ds(p * 40 + f * 8, 8), :]
            for slot, low, high in ((own, 0, 96), (before, 96, 104), (after, 104, 112)):
                target = out_ref.at[pl.ds(pl.multiple_of(slot * 40 + f * 8, 8), 8), :]
                pltpu.store(target, tile, mask=(lane >= low) & (lane < high))
    for copy in stores:
        copy.wait()


def coarse_kernel(coarse_ref, low_ref, high_ref, next_ref, ylow_ref, yhigh_ref, zlow_ref, xedge_ref, carry):
    step = 0.5 * time_step
    rows = lax.broadcasted_iota(jnp.int32, (ZC, LN), 0)
    values = [low_ref[pl.ds(f * ZC, ZC), :] for f in range(NF)]
    for i, v in enumerate(side_of_face(values, primitives(values), 1)):
        carry[i] = v

    def store(ref, f, x, value):
        ref[pl.ds(pl.multiple_of(f * 256 + x * ZC, ZC), ZC), :] = value

    def plane(x, unused):
        cells = [coarse_ref[pl.ds(pl.multiple_of(f * 256 + x * ZC, ZC), ZC), :] for f in range(NF)]
        prims = primitives(cells)
        here = side_of_face(cells, prims, 1)
        flux_x = face_flux([carry[i] for i in range(11)], here)

        @pl.when(x > 0)
        def _():
            for f in range(NF):
                store(next_ref, f, x - 1, carry[11 + f] - step * flux_x[f])

        @pl.when(x == 0)
        def _():
            for f in range(NF):
                xedge_ref[pl.ds(f * 64, ZC), :] = flux_x[f]

        for i in range(11):
            carry[i] = here[i]
        here = side_of_face(cells, prims, 3)
        left = [pltpu.roll(v, 1, 0) for v in here]
        lower_z = face_flux(left, here)
        here = side_of_face(cells, prims, 2)
        left = [pltpu.roll(v, 1, 1) for v in here]
        lower_y = face_flux(left, here)
        for f in range(NF):
            upper_y = pltpu.roll(lower_y[f], LN - 1, 1)
            change = (pltpu.roll(lower_z[f], ZC - 1, 0) - lower_z[f]) + (upper_y - lower_y[f])
            carry[11 + f] = cells[f] - step * (change - flux_x[f])
            store(ylow_ref, f, x, lower_y[f])
            store(yhigh_ref, f, x, upper_y)
            store(zlow_ref, f, x, lower_z[f])
        return unused

    lax.fori_loop(0, CW, plane, 0)
    values = [high_ref[pl.ds(f * ZC, ZC), :] for f in range(NF)]
    flux_x = face_flux([carry[i] for i in range(11)], side_of_face(values, primitives(values), 1))
    for f in range(NF):
        store(next_ref, f, CW - 1, carry[11 + f] - step * flux_x[f])
        xedge_ref[pl.ds(f * 64 + ZC, ZC), :] = flux_x[f]


def apply_kernel(count, box_ref, flag_ref, result_ref, base_ref, ylow_ref, yhigh_ref, zlow_ref, xedge_ref, out_ref):
    me = lax.axis_index("box")
    per_device = ZC // CW * YB
    lane = lanes()
    sub = lax.broadcasted_iota(jnp.int32, (8, LN), 0)
    out_ref[...] = base_ref[...]

    def weight(row, face):
        return flag_ref[row, face].astype(jnp.float32) * (time_step if face % 2 else -time_step)

    def one(source, unused):
        found, rows = find_slots(box_ref, source, me, count, per_device)
        row0 = pl.multiple_of(source * 40, 8)

        def tile(f):
            return result_ref[pl.ds(row0 + f * 8, 8), :]

        for upper in range(2):
            place = found[1 + upper]

            @pl.when(place >= 0)
            def _():
                z0, y0 = anchors(place)
                scale = weight(rows[1 + upper], upper)
                inside = (lane >= y0) & (lane < y0 + CW)
                for f in range(NF):
                    moved = roll_to(tile(f), y0 - 96 - 8 * upper)
                    plane = 0 if upper else CW - 1
                    at = pl.ds(pl.multiple_of(f * 256 + plane * ZC + z0, 8), 8)
                    edge = xedge_ref[pl.ds(pl.multiple_of(f * 64 + (1 - upper) * ZC + z0, 8), 8), :]
                    old = out_ref[at, :]
                    out_ref[at, :] = jnp.where(inside, old + scale * (moved - 0.5 * edge), old)

        place = found[0]

        @pl.when(place >= 0)
        def _():
            z0, y0 = anchors(place)
            inside = (lane >= y0) & (lane < y0 + CW)
            for upper in range(2):
                scale = weight(rows[0], 2 + upper)
                target = (z0 + (CW if upper else -1)) & (ZC - 1)
                face = target if upper else z0
                for f in range(NF):
                    moved = roll_to(tile(f), y0 - 80 - 8 * upper)
                    at = pl.ds(f * 256 + target, 8, stride=ZC)
                    edge = zlow_ref[pl.ds(f * 256 + face, 8, stride=ZC), :]
                    old = out_ref[at, :]
                    out_ref[at, :] = jnp.where(inside, old + scale * (moved - 0.5 * edge), old)
            before = lane == ((y0 - 1) & (LN - 1))
            after = lane == ((y0 + CW) & (LN - 1))
            index = jnp.where(inside, sub * CW + (lane - y0), jnp.where(before, 64 + sub, 72 + sub))
            scale = jnp.where(before, weight(rows[0], 4), jnp.where(after, weight(rows[0], 5), 0.0))
            for f in range(NF):
                for x in range(CW):
                    at = pl.ds(pl.multiple_of(f * 256 + x * ZC + z0, 8), 8)
                    line = jnp.broadcast_to(result_ref[pl.ds(row0 + f * 8 + x, 1), :], (8, LN))
                    got = take_lanes(line, index)
                    edge = jnp.where(before, yhigh_ref[at, :], ylow_ref[at, :])
                    out_ref[at, :] = jnp.where(inside, got, out_ref[at, :] + scale * (got - 0.5 * edge))

        return unused

    lax.fori_loop(0, count, one, 0)


def local(coarse_state, fine_state, patch_box, face_flags):
    count = lax.axis_size("box")
    assert coarse_state.shape == (NF, CW, ZC, LN) and fine_state.shape == (NP, NF, FW, FW * FW)
    coarse = coarse_state.reshape(NF * CW * ZC, LN)
    fine = fine_state.reshape(NP * NF * FW, FW * FW)
    f32 = jnp.float32
    vmem = pl.BlockSpec(memory_space=pltpu.VMEM)
    anywhere = pl.BlockSpec(memory_space=pl.ANY)
    smem = pl.BlockSpec(memory_space=pltpu.SMEM)

    def shaped(*shape):
        return jax.ShapeDtypeStruct(shape, f32)

    def cost(flops, size):
        return pl.CostEstimate(flops=flops, bytes_accessed=size, transcendentals=0)

    packets, first, last = pl.pallas_call(
        functools.partial(pack_kernel, count),
        out_shape=(shaped(count * 16, LN), shaped(NF * ZC, LN), shaped(NF * ZC, LN)),
        in_specs=[smem, vmem],
        out_specs=(vmem, vmem, vmem),
        cost_estimate=cost(1000000, 1000000),
        name="pack",
    )(patch_box, coarse)
    arrived = lax.all_to_all(packets.reshape(count, 16, LN), "box", split_axis=0, concat_axis=0, tiled=True)
    ring = [(i, (i + 1) % count) for i in range(count)]
    low = lax.ppermute(last, "box", ring)
    high = lax.ppermute(first, "box", [(b, a) for a, b in ring])
    fine_next, outbox = pl.pallas_call(
        functools.partial(fine_kernel, count),
        out_shape=(shaped(NP * NF * FW, FW * FW), shaped(count * 40, LN)),
        in_specs=[smem, vmem, anywhere],
        out_specs=(anywhere, vmem),
        scratch_shapes=[
            pltpu.VMEM((NP * 16, LN), f32),
            pltpu.VMEM((11, CW, 8, LN), f32),
            pltpu.VMEM((11, CW, 2, 8, LN), f32),
            pltpu.VMEM((2, 11, 2, 8, LN), f32),
            pltpu.VMEM((NF, FW + 1, 2, 8, LN), f32),
            pltpu.VMEM((16, 2, 8, LN), f32),
            pltpu.VMEM((NF, CW, 8, LN), f32),
            pltpu.VMEM((NF, CW, 2, 8, LN), f32),
            pltpu.VMEM((2, NF, 2, 8, LN), f32),
            pltpu.VMEM((NP * 40, LN), f32),
            pltpu.VMEM((2, NP * NF * FW, LN), f32),
            pltpu.SemaphoreType.DMA((4,)),
        ],
        cost_estimate=cost(20000000, 4000000),
        name="fine",
    )(patch_box, arrived.reshape(count * 16, LN), fine)
    returned = lax.all_to_all(outbox.reshape(count, 40, LN), "box", split_axis=0, concat_axis=0, tiled=True)
    size = NF * CW * ZC
    base, ylow, yhigh, zlow, xedge = pl.pallas_call(
        coarse_kernel,
        out_shape=(shaped(size, LN),) * 4 + (shaped(NF * 2 * ZC, LN),),
        in_specs=[vmem] * 3,
        out_specs=(vmem,) * 5,
        scratch_shapes=[pltpu.VMEM((16, ZC, LN), f32)],
        cost_estimate=cost(10000000, 4000000),
        name="coarse",
    )(coarse, low, high)
    coarse_next = pl.pallas_call(
        functools.partial(apply_kernel, count),
        out_shape=shaped(size, LN),
        in_specs=[smem, smem] + [vmem] * 6,
        out_specs=vmem,
        cost_estimate=cost(2000000, 4000000),
        name="apply",
    )(patch_box, face_flags, returned.reshape(count * 40, LN), base, ylow, yhigh, zlow, xedge)
    return coarse_next.reshape(coarse_state.shape), fine_next.reshape(fine_state.shape)


def solution(mesh):
    placed = (
        P(None, "box", "grp", None),
        P(("grp", "box"), None, None, None),
        P("grp"),
        P("grp", None),
    )
    return jax.shard_map(
        local,
        mesh=mesh,
        in_specs=placed,
        out_specs=(P(None, "box", "grp", None), P(("grp", "box"), None, None, None)),
        check_vma=False,
    )
```

profile of v0, /device:TPU:0, one launch (start us, length us, event | category | flops | bytes accessed | tf_op | source)
XLA Modules:
  0.0 64.1 jit_solution(8287916008584133331)
XLA Ops:
  0.6 4.7 %pack.1 = (f32[256,128]{1,0:T(8,128)}, f32[160,128]{1,0:T(8,128)}, f32[160,128]{1,0:T(8,128)}) custom-call(s32[128]{0:T(128)} %box_ref.5, f32[1280,128]{1,0:T(8,128)} %bitcast.8), custom_call_target="tpu_custom_call" | custom-call | flops 1000000 | bytes 1000000 | tf_op jit(solution)/shard_map/pack/pallas_call | solution.py:498
  5.4 15.3 %all_to_all.10 = f32[16,16,128]{2,1,0:T(8,128)} all-to-all(f32[16,16,128]{2,1,0:T(8,128)} %bitcast.15), channel_id=1, replica_groups=mesh['grp'=2,'box'=16] {'box'}, dimensions={0} | all-to-all | bytes 262144 | tf_op jit(solution)/shard_map/all_to_all | solution.py:506
  20.6 15.1 %fine.1 = (f32[640,256]{1,0:T(8,128)}, f32[640,128]{1,0:T(8,128)}) custom-call(s32[128]{0:T(128)} %box_ref.5, f32[256,128]{1,0:T(8,128)} %bitcast.13, f32[640,256]{1,0:T(8,128)} %bitcast.11), custom_call_target="tpu_custom_call" | custom-call | flops 20000000 | bytes 4000000 | tf_op jit(solution)/shard_map/fine/pallas_call | solution.py:510
  35.7 0.0 copy-start.5
  35.8 0.0 copy-start.4
  35.8 0.0 copy-start.3
  35.8 3.7 %all-to-all-start.1 = ((f32[16,40,128]{2,1,0:T(8,128)}), f32[16,40,128]{2,1,0:T(8,128)S(1)}, u32[]{:S(2)}, u32[]{:S(2)}) async-start(f32[16,40,128]{2,1,0:T(8,128)} %bitcast.14), calls=%async_computation.1 | async-start | bytes 655360 | tf_op jit(solution)/shard_map/all_to_all | solution.py:532
  39.5 0.0 copy-done.5
  39.5 0.3 collective-permute-start
  39.8 0.0 copy-done.4
  39.8 4.2 %collective-permute-start.1 = (f32[160,128]{1,0:T(8,128)S(1)}, f32[160,128]{1,0:T(8,128)S(1)}, u32[]{:S(2)}, u32[]{:S(2)}) collective-permute-start(f32[160,128]{1,0:T(8,128)S(1)} %copy-done.4), channel_id=1, source_target_pairs={{1,0},{2,1},{3,2},{4,3},{5,4},{6,5},{7,6},{8,7},{9,8},{10,9},{11,1... | collective-permute-start | bytes 245768 | tf_op jit(solution)/shard_map/ppermute | solution.py:509
  44.0 0.0 copy-done.3
  44.0 0.7 %copy.6.flag_ref = s32[128,6]{1,0:T(8,128)} copy(s32[128,6]{0,1:T(8,128)S(1)} %copy-done.3) | data formatting | bytes 6144 | tf_op args[3]
  44.7 6.7 %collective-permute-done.low_ref = f32[160,128]{1,0:T(8,128)S(1)} collective-permute-done((f32[160,128]{1,0:T(8,128)S(1)}, f32[160,128]{1,0:T(8,128)S(1)}, u32[]{:S(2)}, u32[]{:S(2)}) %collective-permute-start) | collective-permute-done | bytes 81952 | tf_op jit(solution)/shard_map/ppermute | solution.py:508
  51.4 0.0 copy-start.1
  51.4 0.0 collective-permute-done.1.high_ref
  51.4 0.6 copy-done.1
  52.0 0.0 copy-start.2
  52.0 0.6 copy-done.2
  52.6 4.5 %coarse.1 = (f32[1280,128]{1,0:T(8,128)}, f32[1280,128]{1,0:T(8,128)}, f32[1280,128]{1,0:T(8,128)}, f32[1280,128]{1,0:T(8,128)}, f32[320,128]{1,0:T(8,128)}) custom-call(f32[1280,128]{1,0:T(8,128)} %bitcast.9, f32[160,128]{1,0:T(8,128)} %copy-done.1, f32[160,128]{1,0:T(8,128)} %copy-done.2), custom_call_target="tpu_custom_call" | custom-call | flops 10000000 | bytes 4000000 | tf_op jit(solution)/shard_map/coarse/pallas_call | solution.py:534
  57.1 0.0 all-to-all-done.1
  57.1 0.0 copy-start
  57.1 0.7 %copy-done = f32[16,40,128]{2,1,0:T(8,128)} copy-done((f32[16,40,128]{2,1,0:T(8,128)}, f32[16,40,128]{2,1,0:T(8,128)S(1)}, u32[]{:S(2)}) %copy-start) | copy-done | bytes 327704
  57.9 6.2 %apply.1 = f32[1280,128]{1,0:T(8,128)} custom-call(s32[128]{0:T(128)} %box_ref.5, s32[128,6]{1,0:T(8,128)} %copy.6.flag_ref, f32[640,128]{1,0:T(8,128)} %bitcast.10, f32[1280,128]{1,0:T(8,128)} %get-tuple-element.16.base_ref, f32[1280,128]{1,0:T(8,128)} %get-tuple-element.17.ylow_ref, f32[1280,128]{1,0:T(8,128)} %get-tuple-element.18.yhigh_ref, ...), custom_call_target="tpu_custom_call" | custom-call | flops 2000000 | bytes 4000000 | tf_op jit(solution)/shard_map/apply/pallas_call | solution.py:543
Async XLA Ops:
  35.7 3.7 %copy-start.5 = (f32[160,128]{1,0:T(8,128)S(1)}, f32[160,128]{1,0:T(8,128)}, u32[]{:S(2)}) copy-start(f32[160,128]{1,0:T(8,128)} %get-tuple-element.14) | copy-start | bytes 245764
  35.8 4.1 %copy-start.4 = (f32[160,128]{1,0:T(8,128)S(1)}, f32[160,128]{1,0:T(8,128)}, u32[]{:S(2)}) copy-start(f32[160,128]{1,0:T(8,128)} %get-tuple-element.15) | copy-start | bytes 245764
  35.8 8.2 %copy-start.3 = (s32[128,6]{0,1:T(8,128)S(1)}, s32[128,6]{0,1:T(8,128)}, u32[]{:S(2)}) copy-start(s32[128,6]{0,1:T(8,128)} %param.7) | copy-start | bytes 9220
  35.8 21.4 %all-to-all-start.1 = ((f32[16,40,128]{2,1,0:T(8,128)}), f32[16,40,128]{2,1,0:T(8,128)S(1)}, u32[]{:S(2)}, u32[]{:S(2)}) async-start(f32[16,40,128]{2,1,0:T(8,128)} %bitcast.14), calls=%async_computation.1 | async-start | bytes 655360 | tf_op jit(solution)/shard_map/all_to_all | solution.py:532
  39.5 11.9 %collective-permute-start = (f32[160,128]{1,0:T(8,128)S(1)}, f32[160,128]{1,0:T(8,128)S(1)}, u32[]{:S(2)}, u32[]{:S(2)}) collective-permute-start(f32[160,128]{1,0:T(8,128)S(1)} %copy-done.5), channel_id=1, source_target_pairs={{0,1},{1,2},{2,3},{3,4},{4,5},{5,6},{6,7},{7,8},{8,9},{9,10},{10,1... | collective-permute-start | bytes 245768 | tf_op jit(solution)/shard_map/ppermute | solution.py:508
  39.8 11.6 %collective-permute-start.1 = (f32[160,128]{1,0:T(8,128)S(1)}, f32[160,128]{1,0:T(8,128)S(1)}, u32[]{:S(2)}, u32[]{:S(2)}) collective-permute-start(f32[160,128]{1,0:T(8,128)S(1)} %copy-done.4), channel_id=1, source_target_pairs={{1,0},{2,1},{3,2},{4,3},{5,4},{6,5},{7,6},{8,7},{9,8},{10,9},{11,1... | collective-permute-start | bytes 245768 | tf_op jit(solution)/shard_map/ppermute | solution.py:509
  51.4 0.6 copy-start.1
  52.0 0.6 copy-start.2
  57.1 0.8 %copy-start = (f32[16,40,128]{2,1,0:T(8,128)}, f32[16,40,128]{2,1,0:T(8,128)S(1)}, u32[]{:S(2)}) copy-start(f32[16,40,128]{2,1,0:T(8,128)S(1)} %all-to-all-done.1) | copy-start | bytes 983044
where the time goes:
time: 65.2 us; the launch traced here: 64.1 us
  Pallas kernels  30.5 us (47%)
  blocking collectives  15.3 us (23%)
  starting transfers between devices  8.18 us (13%)
  waiting for transfers between devices  6.68 us (10%)
  local copies, waits for them, and re-layouts  2.74 us (4%)
  between operations  0.69 us (1%)
    all_to_all x1, blocking collectives, local(): lax.all_to_all(packets.reshape(count, 16, LN), 'box', split_axis=0, conca...  15.3 us
    pallas_call x1, Pallas kernels, local(): pl.pallas_call(functools.partial(fine_kernel, count), out_shape=(shaped(N...  15.1 us
    ppermute x1, waiting for transfers between devices, local(): low = lax.ppermute(last, 'box', ring)  6.67 us
    pallas_call x1, Pallas kernels, local(): pl.pallas_call(functools.partial(apply_kernel, count), out_shape=shaped(s...  6.17 us
    pallas_call x1, Pallas kernels, local(): pl.pallas_call(functools.partial(pack_kernel, count), out_shape=(shaped(c...  4.75 us
    pallas_call x1, Pallas kernels, local(): pl.pallas_call(coarse_kernel, out_shape=(shaped(size, LN),) * 4 + (shaped...  4.49 us
    ppermute x1, starting transfers between devices, local(): high = lax.ppermute(first, 'box', [(b, a) for a, b in ring])  4.16 us
    all_to_all x1, starting transfers between devices, local(): lax.all_to_all(outbox.reshape(count, 40, LN), 'box', split_axis=0, concat...  3.69 us
  transfers between devices with their start and end apart: 3, of which 1 were waited for; matrix products, arithmetic and copies ran while one was open for 1% of the time, Pallas kernels for 7%

commit v1 on v0

v1 whole, which is shorter than its diff:
```python
import functools

import jax
import jax.numpy as jnp
from jax import lax
from jax.experimental import pallas as pl
from jax.experimental.pallas import tpu as pltpu
from jax.sharding import PartitionSpec as P


gas_gamma = 1.4
time_step = 0.05

NF = 5
CW = 8
FW = 16
NP = 8
LN = 128
ZC = 32
YB = LN // CW
SIDE = ((0, 0), (0, 33), (0, 66), (1, 0), (1, 33))
XUNIT = tuple((0, 99 + 8 * u) if u < 3 else (1, 66 + 8 * (u - 3)) for u in range(10))


def take_lanes(values, index):
    return jnp.take_along_axis(values, index, axis=1, mode="promise_in_bounds")


def lanes():
    return lax.broadcasted_iota(jnp.int32, (8, LN), 1)


def roll_to(values, shift):
    if isinstance(shift, int):
        shift = shift % LN
        return values if shift == 0 else pltpu.roll(values, shift, 1)
    return pltpu.roll(values, shift & (LN - 1), 1)


def primitives(state):
    inverse = 1.0 / state[0]
    speeds = [None] + [state[m] * inverse for m in (1, 2, 3)]
    squares = state[1] * speeds[1] + state[2] * speeds[2] + state[3] * speeds[3]
    pressure = (gas_gamma - 1.0) * (state[4] - 0.5 * squares)
    sound = jnp.sqrt(gas_gamma * pressure * inverse)
    return speeds, pressure, sound, state[4] + pressure


def side_of_face(state, prims, m):
    speeds, pressure, sound, total = prims
    v = speeds[m]
    flux = [state[m], state[1] * v, state[2] * v, state[3] * v, total * v]
    flux[m] = flux[m] + pressure
    return list(state) + flux + [jnp.abs(v) + sound]


def face_flux(left, right):
    fastest = jnp.maximum(left[10], right[10])
    return [left[5 + f] + right[5 + f] - fastest * (right[f] - left[f]) for f in range(NF)]


def split_box(number, per_device):
    if per_device & (per_device - 1) == 0:
        return number >> (per_device.bit_length() - 1), number & (per_device - 1)
    owner = lax.div(number, jnp.int32(per_device))
    return owner, number - owner * per_device


def fill_slots(box_ref, slot_ref, own_ref, me, count, per_device):
    def clear(i, unused):
        for k in range(3):
            slot_ref[k * count + i] = jnp.int32(-1)
        return unused

    lax.fori_loop(0, count, clear, 0)

    def one(source, used):
        for j in range(NP):
            row = source * NP + j
            owner, _ = split_box(box_ref[row], per_device)
            k = owner - me + 1
            k = jnp.where(k < 0, k + count, k)
            k = jnp.where(k >= count, k - count, k)
            slot_ref[jnp.minimum(k, 3) * count + source] = row
            own_ref[1 + used] = row
            used = used + jnp.where(k == 1, 1, 0)
        return used

    own_ref[0] = lax.fori_loop(0, count, one, 0)


def place_of(box_ref, row, per_device):
    return split_box(box_ref[jnp.maximum(row, 0)], per_device)[1]


def anchors(place):
    return (place >> 4) * CW, (place & (YB - 1)) * CW


def pack_kernel(count, box_hbm, coarse_hbm, out_ref, first_ref, last_ref, slot_ref, own_ref, box_ref, turned, semaphores):
    me = lax.axis_index("box")
    per_device = ZC // CW * YB
    lane = lanes()
    numbers = pltpu.make_async_copy(box_hbm, box_ref, semaphores.at[0])
    numbers.start()
    copies = [
        pltpu.make_async_copy(coarse_hbm.at[:, 0], first_ref, semaphores.at[1]),
        pltpu.make_async_copy(coarse_hbm.at[:, CW - 1], last_ref, semaphores.at[2]),
    ]
    for x in range(CW):
        copies.append(pltpu.make_async_copy(coarse_hbm.at[:, x], turned.at[:, :, x, :], semaphores.at[3 + x]))
    for copy in copies:
        copy.start()
    numbers.wait()
    fill_slots(box_ref, slot_ref, own_ref, me, count, per_device)
    for copy in copies:
        copy.wait()
    spot = jnp.where((lane >= 16) & (lane < 24), lane - 16, jnp.where((lane >= 25) & (lane < 33), lane - 25, -1))

    def edges(block, unused):
        for i in range(4):
            source = block * 4 + i
            before, after = slot_ref[source], slot_ref[2 * count + source]
            ends = [anchors(place_of(box_ref, row, per_device)) for row in (after, before)]
            tiles = [jnp.zeros((8, LN), jnp.float32)] * 2
            for u in range(10):
                f, upper = u // 2, u % 2
                z0, y0 = ends[upper]
                values = (first_ref if upper else last_ref)[f, pl.ds(pl.multiple_of(z0, 8), 8), :]
                tile, base = XUNIT[u]
                moved = roll_to(values, base - y0)
                tiles[tile] = jnp.where(lane >= base, moved, tiles[tile])
            row0 = pl.multiple_of(source * 16, 16)
            out_ref[pl.ds(row0, 8), :] = tiles[0]
            out_ref[pl.ds(row0 + 8, 8), :] = tiles[1]
        return unused

    lax.fori_loop(0, count // 4, edges, 0)

    def faces(pair, unused):
        for i in range(2):
            own = own_ref[1 + jnp.minimum(2 * pair + i, used - 1)]
            row0 = pl.multiple_of(own // NP * 16, 16)
            z0, y0 = anchors(place_of(box_ref, own, per_device))
            below = (z0 - 1) & (ZC - 1)
            above = (z0 + CW) & (ZC - 1)
            sides = [None, None]
            pieces = []
            for f in range(NF):
                piece = jnp.where(lane < 8, roll_to(turned[f, below], -y0), roll_to(turned[f, above], 8 - y0))
                for k in range(CW):
                    piece = jnp.where(spot == k, roll_to(turned[f, z0 + k], 17 + k - y0), piece)
                pieces.append(piece)
            for f in range(NF):
                tile, base = SIDE[f]
                piece = roll_to(pieces[f], base)
                sides[tile] = piece if base == 0 else jnp.where(lane >= base, piece, sides[tile])
            pltpu.store(out_ref.at[pl.ds(row0, 8), :], sides[0], mask=lane < 99)
            pltpu.store(out_ref.at[pl.ds(row0 + 8, 8), :], sides[1], mask=lane < 66)
        return unused

    used = own_ref[0]
    lax.fori_loop(0, (used + 1) // 2, faces, 0)


def spread_kernel(fine_ref, out_ref, semaphores):
    copies = [
        pltpu.make_async_copy(
            fine_ref.at[p, :, :, pl.ds(c * LN, LN)], out_ref.at[:, :, c, p, :], semaphores.at[p * 2 + c]
        )
        for p in range(NP)
        for c in range(2)
    ]
    for copy in copies:
        copy.start()
    for copy in copies:
        copy.wait()


def collect_kernel(state_ref, out_ref, semaphores):
    copies = [
        pltpu.make_async_copy(
            state_ref.at[:, pl.ds(1, FW), c, p, :], out_ref.at[p, :, :, pl.ds(c * LN, LN)], semaphores.at[p * 2 + c]
        )
        for p in range(NP)
        for c in range(2)
    ]
    for copy in copies:
        copy.start()
    for copy in copies:
        copy.wait()


def fine_kernel(
    count,
    box_ref,
    ghost_ref,
    given_ref,
    out_ref,
    last_ref,
    message,
    rows,
    zghost,
    yghost,
    xghost,
    middle,
    carry,
    zsum,
    ysum,
    xsum,
    xpool,
    packed,
):
    per_device = ZC // CW * YB
    me = lax.axis_index("box")
    lane = lanes()
    place_y = lane & 15
    first_y = place_y == 0
    last_y = place_y == 15
    low16 = lane < 16
    high16 = lane < 112

    def slots(p):
        owner, _ = split_box(box_ref[me * NP + p], per_device)
        return owner, jnp.where(owner == 0, count - 1, owner - 1), jnp.where(owner == count - 1, 0, owner + 1)

    for p in range(NP):
        own, before, after = slots(p)
        for tile in range(2):
            start = 99 if tile == 0 else 66
            lower_parity = 0 if tile == 0 else 1
            is_x = lane >= start
            is_lower = (((lane - start) >> 3) & 1) == lower_parity
            pieces = [ghost_ref[pl.ds(pl.multiple_of(s * 16 + tile * 8, 8), 8), :] for s in (own, before, after)]
            message[pl.ds(p * 16 + tile * 8, 8), :] = jnp.where(
                is_x, jnp.where(is_lower, pieces[1], pieces[2]), pieces[0]
            )
    for i in range(16):
        rows[i] = message[pl.ds(i, NP, stride=16), :]
    pair_y = place_y >> 1
    for f in range(NF):
        tile, base = SIDE[f]
        index = jnp.where(lane < 64, base, base + 8) + pair_y
        for r in range(CW):
            zghost[f, r] = take_lanes(rows[tile * 8 + r], index)
        for c in range(2):
            index = jnp.where(place_y < 8, base + 16, base + 25) + (lane >> 5) + 4 * c
            for r in range(CW):
                yghost[f, c, r] = take_lanes(rows[tile * 8 + r], index)
    dense = {}
    for c in range(2):
        for f in range(NF):
            (tile_low, low), (tile_high, high) = XUNIT[2 * f], XUNIT[2 * f + 1]
            for k in range(4):
                moved = roll_to(rows[tile_low * 8 + 4 * c + k], 32 * k - low)
                if (tile_high, high) != (tile_low, low + 8):
                    other = roll_to(rows[tile_high * 8 + 4 * c + k], 32 * k + 8 - high)
                    moved = jnp.where((lane & 15) < 8, moved, other)
                dense[c, f] = moved if k == 0 else jnp.where(lane >= 32 * k, moved, dense[c, f])
    for upper in range(2):
        unfold = (lane & 96) + pair_y + 8 * upper
        for c in range(2):
            for f in range(NF):
                xghost[upper, f, c] = take_lanes(dense[c, f], unfold)
    for half in range(2):
        some = pl.ds(4 * half, 4)
        values = [zghost[f, some] for f in range(NF)]
        for i, v in enumerate(side_of_face(values, primitives(values), 3)[NF:]):
            zghost[NF + i, some] = v
        for c in range(2):
            values = [yghost[f, c, some] for f in range(NF)]
            for i, v in enumerate(side_of_face(values, primitives(values), 2)[NF:]):
                yghost[NF + i, c, some] = v
    for upper in range(2):
        values = [xghost[upper, f] for f in range(NF)]
        for i, v in enumerate(side_of_face(values, primitives(values), 1)[NF:]):
            xghost[upper, NF + i] = v

    step = 0.5 * time_step

    def substep(first):
        target = middle if first else last_ref

        def finish(plane, part, flux):
            for c in range(2):
                for f in range(NF):
                    target[f, plane, c] = part[c][f] - step * flux[c][f]

        for c in range(2):
            for i in range(11):
                carry[i, c] = xghost[0, i, c]
            for f in range(NF):
                carry[11 + f, c] = jnp.zeros((8, LN), jnp.float32)

        def pair(r, unused):
            zg = [zghost[i, r] for i in range(11)]
            zb = [None] * NF
            yb = [[None] * NF for _ in range(2)]
            for half in range(2):
                x = 2 * r + half
                if first:
                    cells = [[given_ref[f, x, c] for f in range(NF)] for c in range(2)]
                else:
                    cells = [[middle[f, x + 1, c] for f in range(NF)] for c in range(2)]
                prims = [primitives(u) for u in cells]
                flux_x = []
                for c in range(2):
                    here = side_of_face(cells[c], prims[c], 1)
                    behind = [carry[i, c] for i in range(11)]
                    flux_x.append(face_flux(behind, here))
                    for i in range(11):
                        carry[i, c] = here[i]
                finish(x, [[carry[11 + f, c] for f in range(NF)] for c in range(2)], flux_x)

                if half == 0:

                    @pl.when(r == 0)
                    def _():
                        for c in range(2):
                            for f in range(NF):
                                value = flux_x[c][f]
                                xsum[0, f, c] = value if first else xsum[0, f, c] + value

                here = [side_of_face(cells[c], prims[c], 3) for c in range(2)]
                turned = [[roll_to(v, 16) for v in here[c]] for c in range(2)]
                left = [
                    [jnp.where(low16, zg[i], turned[0][i]) for i in range(11)],
                    [jnp.where(low16, turned[0][i], turned[1][i]) for i in range(11)],
                ]
                lower = [face_flux(left[c], here[c]) for c in range(2)]
                last = face_flux(here[1], zg)
                change = [[], []]
                for f in range(NF):
                    back = [roll_to(lower[c][f], -16) for c in range(2)]
                    change[0].append(jnp.where(high16, back[0], back[1]) - lower[0][f])
                    change[1].append(jnp.where(high16, back[1], last[f]) - lower[1][f])
                    edge = jnp.where(lane < 64, lower[0][f], last[f])
                    zb[f] = edge if half == 0 else zb[f] + edge
                for c in range(2):
                    yg = [yghost[i, c, r] for i in range(11)]
                    here = side_of_face(cells[c], prims[c], 2)
                    left = [jnp.where(first_y, yg[i], roll_to(here[i], 1)) for i in range(11)]
                    lower_y = face_flux(left, here)
                    last_flux = face_flux(here, yg)
                    for f in range(NF):
                        upper_y = jnp.where(last_y, last_flux[f], roll_to(lower_y[f], -1))
                        change[c][f] = change[c][f] + (upper_y - lower_y[f])
                        edge = jnp.where(place_y < 8, lower_y[f], last_flux[f])
                        yb[c][f] = edge if half == 0 else yb[c][f] + edge
                for c in range(2):
                    for f in range(NF):
                        carry[11 + f, c] = cells[c][f] - step * (change[c][f] - flux_x[c][f])
            for f in range(NF):
                zsum[f, r] = zb[f] if first else zsum[f, r] + zb[f]
                for c in range(2):
                    ysum[f, r, c] = yb[c][f] if first else ysum[f, r, c] + yb[c][f]
            return unused

        lax.fori_loop(0, CW, pair, 0)
        flux_x = [
            face_flux([carry[i, c] for i in range(11)], [xghost[1, i, c] for i in range(11)]) for c in range(2)
        ]
        finish(FW, [[carry[11 + f, c] for f in range(NF)] for c in range(2)], flux_x)
        for c in range(2):
            for f in range(NF):
                value = flux_x[c][f]
                xsum[1, f, c] = value if first else xsum[1, f, c] + value

    substep(True)
    substep(False)

    odd = (lane & 1) == 1
    odd_z = (lane & 16) == 16
    outer = (place_y == 0) | (place_y == 15)

    def shifted(values, shift):
        return [roll_to(v, shift) for v in values]

    def added(left, right):
        return [a + b for a, b in zip(left, right)]

    def dense(values):
        values = added(values, shifted(values, -1))
        return [jnp.where(odd, b, a) for a, b in zip(values, shifted(values, -7))]

    ends = [xsum[side, f, c] for f in range(NF) for side in range(2) for c in range(2)]
    ends = dense(added(ends, shifted(ends, -16)))
    for i, v in enumerate(ends):
        xpool[i] = v
    for f in range(NF):
        sums = [[last_ref[f, 2 * r + 1, c] + last_ref[f, 2 * r + 2, c] for r in range(CW)] for c in range(2)]
        turned = [shifted(sums[0], -1), shifted(sums[1], 1)]
        average = [jnp.where(odd, sums[1][r] + turned[1][r], sums[0][r] + turned[0][r]) for r in range(CW)]
        average = added(average, shifted(average, -16))
        v = [[ysum[f, r, c] for r in range(CW)] for c in range(2)]
        turned = [shifted(v[1], 1), shifted(v[1], -1)]
        fluxes = [
            jnp.where(outer, v[0][r], jnp.where(place_y < 8, turned[0][r], turned[1][r])) for r in range(CW)
        ]
        fluxes = added(fluxes, shifted(fluxes, 16))
        ends = dense([zsum[f, r] for r in range(CW)])
        for low, part in (
            (18, shifted(ends, 18)),
            (114, shifted(ends, 2)),
            (50, [roll_to(xpool[f * 4 + r // 4], 50 - r % 4 * 32) for r in range(CW)]),
            (82, [roll_to(xpool[f * 4 + 2 + r // 4], 82 - r % 4 * 32) for r in range(CW)]),
        ):
            mask = (lane >= low) & (lane < low + 8)
            fluxes = [jnp.where(mask, part[r], fluxes[r]) for r in range(CW)]
        for r in range(CW):
            row = jnp.where(odd_z, fluxes[r] * 0.0625, average[r] * 0.125)
            packed[pl.ds(f * 8 + r, NP, stride=NF * 8), :] = row

    lower_x = (lane >= 50) & (lane < 58)
    upper_x = (lane >= 82) & (lane < 90)
    others = ~(lower_x | upper_x)
    for p in range(NP):
        own, before, after = slots(p)
        for f in range(NF):
            tile = packed[pl.ds(p * 40 + f * 8, 8), :]
            for slot, mask in ((own, others), (before, lower_x), (after, upper_x)):
                target = out_ref.at[pl.ds(pl.multiple_of(slot * 40 + f * 8, 8), 8), :]
                pltpu.store(target, tile, mask=mask)


def coarse_kernel(coarse_ref, low_ref, high_ref, next_ref, yedge_ref, zedge_ref, xedge_ref, carry):
    step = 0.5 * time_step
    upper_edge = (lax.broadcasted_iota(jnp.int32, (ZC, LN), 1) & (CW - 1)) == CW - 1
    values = [low_ref[pl.ds(f * ZC, ZC), :] for f in range(NF)]
    for i, v in enumerate(side_of_face(values, primitives(values), 1)):
        carry[i] = v

    def store(ref, f, x, value):
        ref[pl.ds(pl.multiple_of(f * 256 + x * ZC, ZC), ZC), :] = value

    def plane(x, unused):
        cells = [coarse_ref[pl.ds(pl.multiple_of(f * 256 + x * ZC, ZC), ZC), :] for f in range(NF)]
        prims = primitives(cells)
        here = side_of_face(cells, prims, 1)
        flux_x = face_flux([carry[i] for i in range(11)], here)

        @pl.when(x > 0)
        def _():
            for f in range(NF):
                store(next_ref, f, x - 1, carry[11 + f] - step * flux_x[f])

        @pl.when(x == 0)
        def _():
            for f in range(NF):
                xedge_ref[pl.ds(f * 64, ZC), :] = 0.5 * flux_x[f]

        for i in range(11):
            carry[i] = here[i]
        here = side_of_face(cells, prims, 3)
        left = [pltpu.roll(v, 1, 0) for v in here]
        lower_z = face_flux(left, here)
        here = side_of_face(cells, prims, 2)
        left = [pltpu.roll(v, 1, 1) for v in here]
        lower_y = face_flux(left, here)
        for f in range(NF):
            upper_y = pltpu.roll(lower_y[f], LN - 1, 1)
            change = (pltpu.roll(lower_z[f], ZC - 1, 0) - lower_z[f]) + (upper_y - lower_y[f])
            carry[11 + f] = cells[f] - step * (change - flux_x[f])
            store(yedge_ref, f, x, 0.5 * jnp.where(upper_edge, upper_y, lower_y[f]))
            for k in range(ZC // CW):
                zedge_ref[pl.ds((f * 4 + k) * 8 + x, 1), :] = 0.5 * lower_z[f][k * CW : k * CW + 1, :]
        return unused

    lax.fori_loop(0, CW, plane, 0)
    values = [high_ref[pl.ds(f * ZC, ZC), :] for f in range(NF)]
    flux_x = face_flux([carry[i] for i in range(11)], side_of_face(values, primitives(values), 1))
    for f in range(NF):
        store(next_ref, f, CW - 1, carry[11 + f] - step * flux_x[f])
        xedge_ref[pl.ds(f * 64 + ZC, ZC), :] = 0.5 * flux_x[f]


def apply_kernel(count, box_ref, flag_ref, slot_ref, result_ref, base_ref, yedge_ref, zedge_ref, xedge_ref, out_ref):
    per_device = ZC // CW * YB
    lane = lanes()
    sub = lax.broadcasted_iota(jnp.int32, (8, LN), 0)
    out_ref[...] = base_ref[...]

    def weight(row, face):
        return flag_ref[row, face].astype(jnp.float32) * (time_step if face % 2 else -time_step)

    def one(source, unused):
        before_row, own, after_row = (slot_ref[k * count + source] for k in range(3))
        row0 = pl.multiple_of(source * 40, 8)

        def tile(f):
            return result_ref[pl.ds(row0 + f * 8, 8), :]

        def unmix(y0, first):
            place = lane - y0
            return (first + (place & 3) * 2 + ((place >> 2) & 1)) & (LN - 1)

        for upper in range(2):
            row = before_row if upper else after_row

            @pl.when(row >= 0)
            def _():
                z0, y0 = anchors(place_of(box_ref, row, per_device))
                scale = weight(row, upper)
                inside = (lane >= y0) & (lane < y0 + CW)
                index = unmix(y0, 82 if upper else 50)
                plane = 0 if upper else CW - 1
                places = [pl.ds(pl.multiple_of(f * 256 + plane * ZC + z0, 8), 8) for f in range(NF)]
                new = []
                for f in range(NF):
                    edge = xedge_ref[pl.ds(pl.multiple_of(f * 64 + (1 - upper) * ZC + z0, 8), 8), :]
                    old = out_ref[places[f], :]
                    new.append(jnp.where(inside, old + scale * (take_lanes(tile(f), index) - edge), old))
                for f in range(NF):
                    out_ref[places[f], :] = new[f]

        @pl.when(own >= 0)
        def _():
            place = place_of(box_ref, own, per_device)
            z0, y0 = anchors(place)
            inside = (lane >= y0) & (lane < y0 + CW)
            below = (z0 - 1) & (ZC - 1)
            above = (z0 + CW) & (ZC - 1)
            for upper, target, face in ((0, below, z0), (1, above, above)):
                scale = weight(own, 2 + upper)
                index = unmix(y0, 114 if upper else 18)
                new = []
                for f in range(NF):
                    edge = zedge_ref[pl.ds(pl.multiple_of(f * 32 + face, 8), 8), :]
                    old = out_ref[pl.ds(f * 256 + target, 8, stride=ZC), :]
                    new.append(jnp.where(inside, old + scale * (take_lanes(tile(f), index) - edge), old))
                for f in range(NF):
                    out_ref[pl.ds(f * 256 + target, 8, stride=ZC), :] = new[f]
            before = lane == ((y0 - 1) & (LN - 1))
            after = lane == ((y0 + CW) & (LN - 1))
            part = (sub & 3) * 32 + (sub >> 2)
            faces = jnp.where(before, part + 16, (sub & 3) * 32 + 31 - (sub >> 2))
            index = jnp.where(inside, part + 2 * ((lane - y0) & 7), faces)
            scale = jnp.where(before, weight(own, 4), jnp.where(after, weight(own, 5), 0.0))
            for f in range(NF):
                places = [pl.ds(pl.multiple_of(f * 256 + x * ZC + z0, 8), 8) for x in range(CW)]
                new = []
                for x in range(CW):
                    line = jnp.broadcast_to(result_ref[pl.ds(row0 + f * 8 + x, 1), :], (8, LN))
                    got = take_lanes(line, index)
                    new.append(jnp.where(inside, got, out_ref[places[x], :] + scale * (got - yedge_ref[places[x], :])))
                for x in range(CW):
                    out_ref[places[x], :] = new[x]

        return unused

    lax.fori_loop(0, count, one, 0)


def local(coarse_state, fine_state, patch_box, face_flags):
    count = lax.axis_size("box")
    assert coarse_state.shape == (NF, CW, ZC, LN) and fine_state.shape == (NP, NF, FW, FW * FW)
    coarse = coarse_state.reshape(NF * CW * ZC, LN)
    f32 = jnp.float32
    vmem = pl.BlockSpec(memory_space=pltpu.VMEM)
    smem = pl.BlockSpec(memory_space=pltpu.SMEM)
    hbm = pl.BlockSpec(memory_space=pltpu.HBM)
    anywhere = pl.BlockSpec(memory_space=pl.ANY)

    def shaped(*shape):
        return jax.ShapeDtypeStruct(shape, f32)

    def call(kernel, out_shape, in_specs, out_specs, flops, size, scratch=(), limit=16):
        return pl.pallas_call(
            kernel,
            out_shape=out_shape,
            in_specs=in_specs,
            out_specs=out_specs,
            scratch_shapes=scratch,
            cost_estimate=pl.CostEstimate(flops=flops, bytes_accessed=size, transcendentals=0),
            compiler_params=pltpu.CompilerParams(vmem_limit_bytes=limit * 1024 * 1024),
        )

    packets, first, last, slots, _ = call(
        functools.partial(pack_kernel, count),
        (
            shaped(count * 16, LN),
            shaped(NF, ZC, LN),
            shaped(NF, ZC, LN),
            jax.ShapeDtypeStruct((4 * count,), jnp.int32),
            jax.ShapeDtypeStruct((count + 2,), jnp.int32),
        ),
        [hbm, hbm],
        (vmem, vmem, vmem, smem, smem),
        1000000,
        1000000,
        (
            pltpu.SMEM((count * NP,), jnp.int32),
            pltpu.VMEM((NF, ZC, CW, LN), f32),
            pltpu.SemaphoreType.DMA((3 + CW,)),
        ),
        limit=63,
    )(patch_box, coarse_state)
    arrived = lax.all_to_all(packets.reshape(count, 16, LN), "box", split_axis=0, concat_axis=0, tiled=True)
    ring = [(i, (i + 1) % count) for i in range(count)]
    low = lax.ppermute(last, "box", ring)
    high = lax.ppermute(first, "box", [(b, a) for a, b in ring])
    given = call(
        spread_kernel, shaped(NF, FW, 2, NP, LN), [hbm], vmem, 1000000, 4000000, (pltpu.SemaphoreType.DMA((2 * NP,)),)
    )(fine_state)
    outbox, state = call(
        functools.partial(fine_kernel, count),
        (shaped(count * 40, LN), shaped(NF, FW + 1, 2, NP, LN)),
        [smem, vmem, vmem],
        (vmem, vmem),
        20000000,
        4000000,
        (
            pltpu.VMEM((NP * 16, LN), f32),
            pltpu.VMEM((16, NP, LN), f32),
            pltpu.VMEM((11, CW, 8, LN), f32),
            pltpu.VMEM((11, 2, CW, 8, LN), f32),
            pltpu.VMEM((2, 11, 2, 8, LN), f32),
            pltpu.VMEM((NF, FW + 1, 2, 8, LN), f32),
            pltpu.VMEM((16, 2, 8, LN), f32),
            pltpu.VMEM((NF, CW, 8, LN), f32),
            pltpu.VMEM((NF, CW, 2, 8, LN), f32),
            pltpu.VMEM((2, NF, 2, 8, LN), f32),
            pltpu.VMEM((4 * NF, NP, LN), f32),
            pltpu.VMEM((NP * 40, LN), f32),
        ),
    )(patch_box, arrived.reshape(count * 16, LN), given)
    returned = lax.all_to_all(outbox.reshape(count, 40, LN), "box", split_axis=0, concat_axis=0, tiled=True)
    fine_next = call(
        collect_kernel,
        shaped(*fine_state.shape),
        [vmem],
        anywhere,
        1000000,
        4000000,
        (pltpu.SemaphoreType.DMA((2 * NP,)),),
    )(state)
    size = NF * CW * ZC
    base, yedge, zedge, xedge = call(
        coarse_kernel,
        (shaped(size, LN), shaped(size, LN), shaped(NF * 32, LN), shaped(NF * 2 * ZC, LN)),
        [vmem] * 3,
        (vmem,) * 4,
        10000000,
        4000000,
        (pltpu.VMEM((16, ZC, LN), f32),),
    )(coarse, low.reshape(NF * ZC, LN), high.reshape(NF * ZC, LN))
    coarse_next = call(
        functools.partial(apply_kernel, count), shaped(size, LN), [smem] * 3 + [vmem] * 5, vmem, 2000000, 4000000
    )(patch_box, face_flags, slots, returned.reshape(count * 40, LN), base, yedge, zedge, xedge)
    return coarse_next.reshape(coarse_state.shape), fine_next


def solution(mesh):
    placed = (
        P(None, "box", "grp", None),
        P(("grp", "box"), None, None, None),
        P("grp"),
        P("grp", None),
    )
    return jax.shard_map(
        local,
        mesh=mesh,
        in_specs=placed,
        out_specs=(P(None, "box", "grp", None), P(("grp", "box"), None, None, None)),
        check_vma=False,
    )
```

time: 65.2 us -> 53.4 us (0.82); the launches traced: 64.1 us -> 53 us
  blocking collectives: 15.3 us -> 0 us
  Pallas kernels: 30.5 us -> 21.1 us
  waiting for transfers between devices: 6.68 us -> 14.5 us
  starting transfers between devices: 8.18 us -> 15.8 us
  local copies, waits for them, and re-layouts: 2.74 us -> 0.81 us
    all_to_all x1 -> x0, blocking collectives: 15.3 us -> none  [local(): lax.all_to_all(packets.reshape(count, 16, LN), 'box', split_axis=0, conca...]
    pallas_call x4 -> x6, Pallas kernels: 30.5 us -> 21.1 us  [the longest x1 8.35 us: local(): call(functools.partial(fine_kernel, count), (shaped(count * 40, LN), shap...]
    all_to_all x0 -> x1, starting transfers between devices: none -> 7.64 us  [local(): lax.all_to_all(packets.reshape(count, 16, LN), 'box', split_axis=0, conca...]
    all_to_all x0 -> x1, waiting for transfers between devices: none -> 7.25 us  [local(): lax.all_to_all(packets.reshape(count, 16, LN), 'box', split_axis=0, conca...]
    unnamed x13 -> x15, local copies, waits for them, and re-layouts: 2.74 us -> 0.81 us
  transfers between devices with their start and end apart: 3 -> 4, of which waited for: 1 -> 2; matrix products, arithmetic and copies ran while one was open for 1% -> 0% of each run, Pallas kernels for 7% -> 7%
where the time goes in v1:
time: 53.4 us; the launch traced here: 53 us
  Pallas kernels  21.1 us (40%)
  starting transfers between devices  15.8 us (30%)
  waiting for transfers between devices  14.5 us (27%)
  local copies, waits for them, and re-layouts  0.81 us (2%)
  between operations  0.73 us (1%)
    pallas_call x1, Pallas kernels, local(): call(functools.partial(fine_kernel, count), (shaped(count * 40, LN), shap...  8.35 us
    all_to_all x1, starting transfers between devices, local(): lax.all_to_all(packets.reshape(count, 16, LN), 'box', split_axis=0, conca...  7.64 us
    ppermute x1, waiting for transfers between devices, local(): low = lax.ppermute(last, 'box', ring)  7.29 us
    all_to_all x1, waiting for transfers between devices, local(): lax.all_to_all(packets.reshape(count, 16, LN), 'box', split_axis=0, conca...  7.25 us
    pallas_call x1, Pallas kernels, local(): call(functools.partial(apply_kernel, count), shaped(size, LN), [smem] * 3...  5.2 us
    ppermute x1, starting transfers between devices, local(): high = lax.ppermute(first, 'box', [(b, a) for a, b in ring])  4.16 us
    pallas_call x1, Pallas kernels, local(): call(functools.partial(pack_kernel, count), (shaped(count * 16, LN), shap...  4.05 us
    all_to_all x1, starting transfers between devices, local(): lax.all_to_all(outbox.reshape(count, 40, LN), 'box', split_axis=0, concat...  3.67 us
  transfers between devices with their start and end apart: 4, of which 2 were waited for; matrix products, arithmetic and copies ran while one was open for 0% of the time, Pallas kernels for 7%

profile of v1, /device:TPU:0, one launch (start us, length us, event | category | flops | bytes accessed | tf_op | source)
XLA Modules:
  0.0 53.0 jit_solution(15486799447781873535)
XLA Ops:
  0.6 0.0 copy-start.1
  0.6 4.0 %shard_map.59 = (f32[256,128]{1,0:T(8,128)}, f32[5,32,128]{2,1,0:T(8,128)}, f32[5,32,128]{2,1,0:T(8,128)}, s32[64]{0:T(128)}, s32[18]{0:T(128)}) custom-call(s32[128]{0:T(128)} %box_ref.3, f32[5,8,32,128]{3,2,1,0:T(8,128)} %coarse_hbm.1), custom_call_target="tpu_custom_call" | custom-call | flops 1000000 | bytes 1000000 | tf_op jit(solution)/shard_map/pallas_call | solution.py:578
  4.7 7.6 %all-to-all-start = ((f32[16,16,128]{2,1,0:T(8,128)}), f32[16,16,128]{2,1,0:T(8,128)S(1)}, u32[]{:S(2)}, u32[]{:S(2)}) async-start(f32[16,16,128]{2,1,0:T(8,128)} %bitcast.14), calls=%async_computation | async-start | bytes 262144 | tf_op jit(solution)/shard_map/all_to_all | solution.py:598
  12.3 0.0 copy-done.1
  12.4 0.6 %shard_map.60.given_ref = f32[5,16,2,8,128]{4,3,2,1,0:T(8,128)S(1)} custom-call(f32[8,5,16,256]{3,2,1,0:T(8,128)S(1)} %copy-done.1), custom_call_target="tpu_custom_call" | custom-call | flops 1000000 | bytes 4000000 | tf_op jit(solution)/shard_map/pallas_call | solution.py:602
  13.0 0.0 copy-start.2
  13.0 7.2 %all-to-all-done = f32[16,16,128]{2,1,0:T(8,128)S(1)} async-done(((f32[16,16,128]{2,1,0:T(8,128)}), f32[16,16,128]{2,1,0:T(8,128)S(1)}, u32[]{:S(2)}, u32[]{:S(2)}) %all-to-all-start) | async-done | bytes 131104 | tf_op jit(solution)/shard_map/all_to_all | solution.py:598
  20.2 0.0 copy-done.2
  20.3 0.0 copy-start
  20.3 8.4 %shard_map.61 = (f32[640,128]{1,0:T(8,128)}, f32[5,17,2,8,128]{4,3,2,1,0:T(8,128)S(1)}) custom-call(s32[128]{0:T(128)S(1)} %copy-done.2, f32[256,128]{1,0:T(8,128)S(1)} %bitcast.10, f32[5,16,2,8,128]{4,3,2,1,0:T(8,128)S(1)} %shard_map.60.given_ref), custom_call_target="tpu_custom_call" | custom-call | flops 20000000 | bytes 4000000 | tf_op jit(solution)/shard_map/pallas_call | solution.py:605
  28.6 0.0 copy-start.6
  28.6 0.0 copy-start.5
  28.6 0.0 copy-start.4
  28.6 3.7 %all-to-all-start.1 = ((f32[16,40,128]{2,1,0:T(8,128)}), f32[16,40,128]{2,1,0:T(8,128)S(1)}, u32[]{:S(2)}, u32[]{:S(2)}) async-start(f32[16,40,128]{2,1,0:T(8,128)} %bitcast.2), calls=%async_computation.1 | async-start | bytes 655360 | tf_op jit(solution)/shard_map/all_to_all | solution.py:627
  32.3 0.0 copy-done.6
  32.3 0.3 collective-permute-start
  32.6 0.0 copy-done.5
  32.6 4.2 %collective-permute-start.1 = (f32[5,32,128]{2,1,0:T(8,128)S(1)}, f32[5,32,128]{2,1,0:T(8,128)S(1)}, u32[]{:S(2)}, u32[]{:S(2)}) collective-permute-start(f32[5,32,128]{2,1,0:T(8,128)S(1)} %copy-done.5), channel_id=1, source_target_pairs={{1,0},{2,1},{3,2},{4,3},{5,4},{6,5},{7,6},{8,7},{9,8},{10,9},{11,1... | collective-permute-start | bytes 245768 | tf_op jit(solution)/shard_map/ppermute | solution.py:601
  36.8 0.0 copy-done.4
  36.8 0.1 copy.6.flag_ref
  36.9 7.3 %collective-permute-done = f32[5,32,128]{2,1,0:T(8,128)S(1)} collective-permute-done((f32[5,32,128]{2,1,0:T(8,128)S(1)}, f32[5,32,128]{2,1,0:T(8,128)S(1)}, u32[]{:S(2)}, u32[]{:S(2)}) %collective-permute-start) | collective-permute-done | bytes 81952 | tf_op jit(solution)/shard_map/ppermute | solution.py:600
  44.2 0.0 collective-permute-done.1
  44.2 0.0 copy-done
  44.2 1.9 %shard_map.62 = (f32[1280,128]{1,0:T(8,128)S(1)}, f32[1280,128]{1,0:T(8,128)S(1)}, f32[160,128]{1,0:T(8,128)S(1)}, f32[320,128]{1,0:T(8,128)S(1)}) custom-call(f32[1280,128]{1,0:T(8,128)S(1)} %bitcast.8, f32[160,128]{1,0:T(8,128)S(1)} %bitcast.11, f32[160,128]{1,0:T(8,128)S(1)} %bitcast.12), custom_call_target="tpu_custom_call" | custom-call | flops 10000000 | bytes 4000000 | tf_op jit(solution)/shard_map/pallas_call | solution.py:638
  46.1 1.0 %shard_map.64 = f32[8,5,16,256]{3,2,1,0:T(8,128)} custom-call(f32[5,17,2,8,128]{4,3,2,1,0:T(8,128)S(1)} %get-tuple-element.21.state_ref), custom_call_target="tpu_custom_call" | custom-call | flops 1000000 | bytes 4000000 | tf_op jit(solution)/shard_map/pallas_call | solution.py:628
  47.1 0.0 all-to-all-done.1
  47.1 0.0 copy-start.3
  47.1 0.7 %copy-done.3 = s32[64]{0:T(128)S(1)} copy-done((s32[64]{0:T(128)S(1)}, s32[64]{0:T(128)}, u32[]{:S(2)}) %copy-start.3) | copy-done | bytes 280
  47.8 5.2 %shard_map.63 = f32[1280,128]{1,0:T(8,128)} custom-call(s32[128]{0:T(128)S(1)} %copy-done.2, s32[128,6]{1,0:T(8,128)S(1)} %copy.6.flag_ref, s32[64]{0:T(128)S(1)} %copy-done.3, f32[640,128]{1,0:T(8,128)S(1)} %bitcast.9, f32[1280,128]{1,0:T(8,128)S(1)} %get-tuple-element.17.base_ref, f32[1280,128]{1,0:T(8,128)S(1)} %get-tuple-element.18.yedge_ref, ...), custom_call_target="tpu_custom_call" | custom-call | flops 2000000 | bytes 4000000 | tf_op jit(solution)/shard_map/pallas_call | solution.py:647
Async XLA Ops:
  0.6 11.7 %copy-start.1 = (f32[8,5,16,256]{3,2,1,0:T(8,128)S(1)}, f32[8,5,16,256]{3,2,1,0:T(8,128)}, u32[]{:S(2)}) copy-start(f32[8,5,16,256]{3,2,1,0:T(8,128)} %fine_ref.1) | copy-start | bytes 1966084
  4.7 15.6 %all-to-all-start = ((f32[16,16,128]{2,1,0:T(8,128)}), f32[16,16,128]{2,1,0:T(8,128)S(1)}, u32[]{:S(2)}, u32[]{:S(2)}) async-start(f32[16,16,128]{2,1,0:T(8,128)} %bitcast.14), calls=%async_computation | async-start | bytes 262144 | tf_op jit(solution)/shard_map/all_to_all | solution.py:598
  13.0 7.3 %copy-start.2 = (s32[128]{0:T(128)S(1)}, s32[128]{0:T(128)}, u32[]{:S(2)}) copy-start(s32[128]{0:T(128)} %box_ref.3) | copy-start | bytes 1540
  20.3 24.0 %copy-start = (f32[5,8,32,128]{3,2,1,0:T(8,128)S(1)}, f32[5,8,32,128]{3,2,1,0:T(8,128)}, u32[]{:S(2)}) copy-start(f32[5,8,32,128]{3,2,1,0:T(8,128)} %coarse_hbm.1) | copy-start | bytes 1966084
  28.6 3.7 %copy-start.6 = (f32[5,32,128]{2,1,0:T(8,128)S(1)}, f32[5,32,128]{2,1,0:T(8,128)}, u32[]{:S(2)}) copy-start(f32[5,32,128]{2,1,0:T(8,128)} %get-tuple-element.15) | copy-start | bytes 245764
  28.6 4.0 %copy-start.5 = (f32[5,32,128]{2,1,0:T(8,128)S(1)}, f32[5,32,128]{2,1,0:T(8,128)}, u32[]{:S(2)}) copy-start(f32[5,32,128]{2,1,0:T(8,128)} %get-tuple-element.16) | copy-start | bytes 245764
  28.6 8.2 %copy-start.4 = (s32[128,6]{0,1:T(8,128)S(1)}, s32[128,6]{0,1:T(8,128)}, u32[]{:S(2)}) copy-start(s32[128,6]{0,1:T(8,128)} %param.7) | copy-start | bytes 9220
  28.6 18.5 %all-to-all-start.1 = ((f32[16,40,128]{2,1,0:T(8,128)}), f32[16,40,128]{2,1,0:T(8,128)S(1)}, u32[]{:S(2)}, u32[]{:S(2)}) async-start(f32[16,40,128]{2,1,0:T(8,128)} %bitcast.2), calls=%async_computation.1 | async-start | bytes 655360 | tf_op jit(solution)/shard_map/all_to_all | solution.py:627
  32.3 11.9 %collective-permute-start = (f32[5,32,128]{2,1,0:T(8,128)S(1)}, f32[5,32,128]{2,1,0:T(8,128)S(1)}, u32[]{:S(2)}, u32[]{:S(2)}) collective-permute-start(f32[5,32,128]{2,1,0:T(8,128)S(1)} %copy-done.6), channel_id=1, source_target_pairs={{0,1},{1,2},{2,3},{3,4},{4,5},{5,6},{6,7},{7,8},{8,9},{9,10},{10,1... | collective-permute-start | bytes 245768 | tf_op jit(solution)/shard_map/ppermute | solution.py:600
  32.6 11.6 %collective-permute-start.1 = (f32[5,32,128]{2,1,0:T(8,128)S(1)}, f32[5,32,128]{2,1,0:T(8,128)S(1)}, u32[]{:S(2)}, u32[]{:S(2)}) collective-permute-start(f32[5,32,128]{2,1,0:T(8,128)S(1)} %copy-done.5), channel_id=1, source_target_pairs={{1,0},{2,1},{3,2},{4,3},{5,4},{6,5},{7,6},{8,7},{9,8},{10,9},{11,1... | collective-permute-start | bytes 245768 | tf_op jit(solution)/shard_map/ppermute | solution.py:601
  47.1 0.7 %copy-start.3 = (s32[64]{0:T(128)S(1)}, s32[64]{0:T(128)}, u32[]{:S(2)}) copy-start(s32[64]{0:T(128)} %get-tuple-element.12.slot_ref) | copy-start | bytes 772

commit v2 on v1

--- a/solution.py
+++ b/solution.py
@@ -73,20 +73,30 @@
         return unused
 
     lax.fori_loop(0, count, clear, 0)
-
-    def one(source, used):
+    power = count & (count - 1) == 0
+    shifted = me - 1
+
+    def one(source, unused):
         for j in range(NP):
             row = source * NP + j
             owner, _ = split_box(box_ref[row], per_device)
-            k = owner - me + 1
-            k = jnp.where(k < 0, k + count, k)
-            k = jnp.where(k >= count, k - count, k)
+            k = owner - shifted
+            if power:
+                k = k & (count - 1)
+            else:
+                k = jnp.where(k < 0, k + count, k)
+                k = jnp.where(k >= count, k - count, k)
             slot_ref[jnp.minimum(k, 3) * count + source] = row
-            own_ref[1 + used] = row
-            used = used + jnp.where(k == 1, 1, 0)
-        return used
-
-    own_ref[0] = lax.fori_loop(0, count, one, 0)
+        return unused
+
+    lax.fori_loop(0, count, one, 0)
+
+    def listed(source, used):
+        row = slot_ref[count + source]
+        own_ref[1 + used] = row
+        return used + jnp.where(row >= 0, 1, 0)
+
+    own_ref[0] = lax.fori_loop(0, count, listed, 0)
 
 
 def place_of(box_ref, row, per_device):
@@ -163,11 +173,14 @@
     lax.fori_loop(0, (used + 1) // 2, faces, 0)
 
 
-def spread_kernel(fine_ref, out_ref, semaphores):
+def interior_kernel(fine_ref, middle_ref, cells_ref, given, carry, semaphores):
+    step = 0.5 * time_step
+    lane = lanes()
+    low16 = lane < 16
+    high16 = lane < 112
+    first_y = (lane & 15) == 0
     copies = [
-        pltpu.make_async_copy(
-            fine_ref.at[p, :, :, pl.ds(c * LN, LN)], out_ref.at[:, :, c, p, :], semaphores.at[p * 2 + c]
-        )
+        pltpu.make_async_copy(fine_ref.at[p, :, :, pl.ds(c * LN, LN)], given.at[:, :, c, p, :], semaphores.at[p * 2 + c])
         for p in range(NP)
         for c in range(2)
     ]
@@ -175,6 +188,56 @@
         copy.start()
     for copy in copies:
         copy.wait()
+    for c in range(2):
+        cells = [given[f, 0, c] for f in range(NF)]
+        for i, v in enumerate(side_of_face(cells, primitives(cells), 1)):
+            carry[i, c] = v
+        for f in range(NF):
+            carry[11 + f, c] = jnp.zeros((8, LN), jnp.float32)
+
+    def pair(r, unused):
+        for half in range(2):
+            x = 2 * r + half
+            cells = [[given[f, x, c] for f in range(NF)] for c in range(2)]
+            prims = [primitives(u) for u in cells]
+            for c in range(2):
+                speeds, pressure, sound, _ = prims[c]
+                for i, v in enumerate(cells[c] + [speeds[2], speeds[3], pressure, sound]):
+                    cells_ref[i, x, c] = v
+            flux_x = []
+            for c in range(2):
+                here = side_of_face(cells[c], prims[c], 1)
+                flux = face_flux([carry[i, c] for i in range(11)], here)
+                if half == 0:
+                    flux = [jnp.where(r == 0, 0.0, v) for v in flux]
+                flux_x.append(flux)
+                for i in range(11):
+                    carry[i, c] = here[i]
+                for f in range(NF):
+                    middle_ref[f, x, c] = carry[11 + f, c] - step * flux[f]
+            here = [side_of_face(cells[c], prims[c], 3) for c in range(2)]
+            turned = [[roll_to(v, 16) for v in here[c]] for c in range(2)]
+            left = [turned[0], [jnp.where(low16, turned[0][i], turned[1][i]) for i in range(11)]]
+            lower = [face_flux(left[c], here[c]) for c in range(2)]
+            lower[0] = [jnp.where(low16, 0.0, v) for v in lower[0]]
+            change = [[], []]
+            for f in range(NF):
+                back = [roll_to(lower[c][f], -16) for c in range(2)]
+                change[0].append(jnp.where(high16, back[0], back[1]) - lower[0][f])
+                change[1].append(jnp.where(high16, back[1], back[0]) - lower[1][f])
+            for c in range(2):
+                here = side_of_face(cells[c], prims[c], 2)
+                lower_y = face_flux([roll_to(v, 1) for v in here], here)
+                lower_y = [jnp.where(first_y, 0.0, v) for v in lower_y]
+                for f in range(NF):
+                    total = change[c][f] + (roll_to(lower_y[f], -1) - lower_y[f]) - flux_x[c][f]
+                    carry[11 + f, c] = cells[c][f] - step * total
+        return unused
+
+    lax.fori_loop(0, CW, pair, 0)
+    for c in range(2):
+        for f in range(NF):
+            middle_ref[f, FW, c] = carry[11 + f, c]
 
 
 def collect_kernel(state_ref, out_ref, semaphores):
@@ -195,7 +258,8 @@
     count,
     box_ref,
     ghost_ref,
-    given_ref,
+    middle_ref,
+    cells_ref,
     out_ref,
     last_ref,
     message,
@@ -278,96 +342,121 @@
 
     step = 0.5 * time_step
 
-    def substep(first):
-        target = middle if first else last_ref
-
-        def finish(plane, part, flux):
+    sign_z = jnp.where(lane < 64, -1.0, 1.0)
+    sign_y = jnp.where(place_y < 8, -1.0, 1.0)
+    scale_z = [jnp.where(low16, step, 0.0), jnp.where(high16, 0.0, -step)]
+    scale_y = jnp.where(first_y, step, jnp.where(last_y, -step, 0.0))
+
+    def outer_flux(inside, ghost, sign):
+        fastest = jnp.maximum(inside[10], ghost[10]) * sign
+        return [inside[5 + f] + ghost[5 + f] - fastest * (ghost[f] - inside[f]) for f in range(NF)]
+
+    def outer_faces(r, unused):
+        both = pl.ds(2 * r, 2)
+        cells = [[cells_ref[i, both, c] for i in range(9)] for c in range(2)]
+
+        def inside(values, m):
+            speeds = [None, None, values[5], values[6]]
+            return side_of_face(values[:NF], (speeds, values[7], values[8], values[4] + values[7]), m)
+
+        edge = [jnp.where(lane < 64, cells[0][i], cells[1][i]) for i in range(9)]
+        flux_z = outer_flux(inside(edge, 3), [zghost[i, r] for i in range(11)], sign_z)
+        for f in range(NF):
+            zsum[f, r] = flux_z[f][0] + flux_z[f][1]
+        for c in range(2):
+            flux_y = outer_flux(inside(cells[c], 2), [yghost[i, c, r] for i in range(11)], sign_y)
+            for f in range(NF):
+                ysum[f, r, c] = flux_y[f][0] + flux_y[f][1]
+                old = middle_ref[f, pl.ds(2 * r + 1, 2), c]
+                middle[f, both, c] = old + flux_y[f] * scale_y + flux_z[f] * scale_z[c]
+        return unused
+
+    lax.fori_loop(0, CW, outer_faces, 0)
+    for side, plane in ((0, 0), (1, FW - 1)):
+        values = [cells_ref[f, plane] for f in range(NF)]
+        sides = [[xghost[side, i] for i in range(11)], side_of_face(values, primitives(values), 1)]
+        flux_x = face_flux(*(sides[::-1] if side else sides))
+        for f in range(NF):
+            xsum[side, f] = flux_x[f]
+            middle[f, plane] = middle[f, plane] + (-step if side else step) * flux_x[f]
+
+    def finish(plane, part, flux):
+        for c in range(2):
+            for f in range(NF):
+                last_ref[f, plane, c] = part[c][f] - step * flux[c][f]
+
+    for c in range(2):
+        for i in range(11):
+            carry[i, c] = xghost[0, i, c]
+        for f in range(NF):
+            carry[11 + f, c] = jnp.zeros((8, LN), jnp.float32)
+
+    def pair(r, unused):
+        zg = [zghost[i, r] for i in range(11)]
+        zb = [None] * NF
+        yb = [[None] * NF for _ in range(2)]
+        for half in range(2):
+            x = 2 * r + half
+            cells = [[middle[f, x, c] for f in range(NF)] for c in range(2)]
+            prims = [primitives(u) for u in cells]
+            flux_x = []
+            for c in range(2):
+                here = side_of_face(cells[c], prims[c], 1)
+                behind = [carry[i, c] for i in range(11)]
+                flux_x.append(face_flux(behind, here))
+                for i in range(11):
+                    carry[i, c] = here[i]
+            finish(x, [[carry[11 + f, c] for f in range(NF)] for c in range(2)], flux_x)
+
+            if half == 0:
+
+                @pl.when(r == 0)
+                def _():
+                    for c in range(2):
+                        for f in range(NF):
+                            xsum[0, f, c] = xsum[0, f, c] + flux_x[c][f]
+
+            here = [side_of_face(cells[c], prims[c], 3) for c in range(2)]
+            turned = [[roll_to(v, 16) for v in here[c]] for c in range(2)]
+            left = [
+                [jnp.where(low16, zg[i], turned[0][i]) for i in range(11)],
+                [jnp.where(low16, turned[0][i], turned[1][i]) for i in range(11)],
+            ]
+            lower = [face_flux(left[c], here[c]) for c in range(2)]
+            last = face_flux(here[1], zg)
+            change = [[], []]
+            for f in range(NF):
+                back = [roll_to(lower[c][f], -16) for c in range(2)]
+                change[0].append(jnp.where(high16, back[0], back[1]) - lower[0][f])
+                change[1].append(jnp.where(high16, back[1], last[f]) - lower[1][f])
+                edge = jnp.where(lane < 64, lower[0][f], last[f])
+                zb[f] = edge if half == 0 else zb[f] + edge
+            for c in range(2):
+                yg = [yghost[i, c, r] for i in range(11)]
+                here = side_of_face(cells[c], prims[c], 2)
+                left = [jnp.where(first_y, yg[i], roll_to(here[i], 1)) for i in range(11)]
+                lower_y = face_flux(left, here)
+                last_flux = face_flux(here, yg)
+                for f in range(NF):
+                    upper_y = jnp.where(last_y, last_flux[f], roll_to(lower_y[f], -1))
+                    change[c][f] = change[c][f] + (upper_y - lower_y[f])
+                    edge = jnp.where(place_y < 8, lower_y[f], last_flux[f])
+                    yb[c][f] = edge if half == 0 else yb[c][f] + edge
             for c in range(2):
                 for f in range(NF):
-                    target[f, plane, c] = part[c][f] - step * flux[c][f]
-
-        for c in range(2):
-            for i in range(11):
-                carry[i, c] = xghost[0, i, c]
-            for f in range(NF):
-                carry[11 + f, c] = jnp.zeros((8, LN), jnp.float32)
-
-        def pair(r, unused):
-            zg = [zghost[i, r] for i in range(11)]
-            zb = [None] * NF
-            yb = [[None] * NF for _ in range(2)]
-            for half in range(2):
-                x = 2 * r + half
-                if first:
-                    cells = [[given_ref[f, x, c] for f in range(NF)] for c in range(2)]
-                else:
-                    cells = [[middle[f, x + 1, c] for f in range(NF)] for c in range(2)]
-                prims = [primitives(u) for u in cells]
-                flux_x = []
-                for c in range(2):
-                    here = side_of_face(cells[c], prims[c], 1)
-                    behind = [carry[i, c] for i in range(11)]
-                    flux_x.append(face_flux(behind, here))
-                    for i in range(11):
-                        carry[i, c] = here[i]
-                finish(x, [[carry[11 + f, c] for f in range(NF)] for c in range(2)], flux_x)
-
-                if half == 0:
-
-                    @pl.when(r == 0)
-                    def _():
-                        for c in range(2):
-                            for f in range(NF):
-                                value = flux_x[c][f]
-                                xsum[0, f, c] = value if first else xsum[0, f, c] + value
-
-                here = [side_of_face(cells[c], prims[c], 3) for c in range(2)]
-                turned = [[roll_to(v, 16) for v in here[c]] for c in range(2)]
-                left = [
-                    [jnp.where(low16, zg[i], turned[0][i]) for i in range(11)],
-                    [jnp.where(low16, turned[0][i], turned[1][i]) for i in range(11)],
-                ]
-                lower = [face_flux(left[c], here[c]) for c in range(2)]
-                last = face_flux(here[1], zg)
-                change = [[], []]
-                for f in range(NF):
-                    back = [roll_to(lower[c][f], -16) for c in range(2)]
-                    change[0].append(jnp.where(high16, back[0], back[1]) - lower[0][f])
-                    change[1].append(jnp.where(high16, back[1], last[f]) - lower[1][f])
-                    edge = jnp.where(lane < 64, lower[0][f], last[f])
-                    zb[f] = edge if half == 0 else zb[f] + edge
-                for c in range(2):
-                    yg = [yghost[i, c, r] for i in range(11)]
-                    here = side_of_face(cells[c], prims[c], 2)
-                    left = [jnp.where(first_y, yg[i], roll_to(here[i], 1)) for i in range(11)]
-                    lower_y = face_flux(left, here)
-                    last_flux = face_flux(here, yg)
-                    for f in range(NF):
-                        upper_y = jnp.where(last_y, last_flux[f], roll_to(lower_y[f], -1))
-                        change[c][f] = change[c][f] + (upper_y - lower_y[f])
-                        edge = jnp.where(place_y < 8, lower_y[f], last_flux[f])
-                        yb[c][f] = edge if half == 0 else yb[c][f] + edge
-                for c in range(2):
-                    for f in range(NF):
-                        carry[11 + f, c] = cells[c][f] - step * (change[c][f] - flux_x[c][f])
-            for f in range(NF):
-                zsum[f, r] = zb[f] if first else zsum[f, r] + zb[f]
-                for c in range(2):
-                    ysum[f, r, c] = yb[c][f] if first else ysum[f, r, c] + yb[c][f]
-            return unused
-
-        lax.fori_loop(0, CW, pair, 0)
-        flux_x = [
-            face_flux([carry[i, c] for i in range(11)], [xghost[1, i, c] for i in range(11)]) for c in range(2)
-        ]
-        finish(FW, [[carry[11 + f, c] for f in range(NF)] for c in range(2)], flux_x)
-        for c in range(2):
-            for f in range(NF):
-                value = flux_x[c][f]
-                xsum[1, f, c] = value if first else xsum[1, f, c] + value
-
-    substep(True)
-    substep(False)
+                    carry[11 + f, c] = cells[c][f] - step * (change[c][f] - flux_x[c][f])
+        for f in range(NF):
+            zsum[f, r] = zsum[f, r] + zb[f]
+            for c in range(2):
+                ysum[f, r, c] = ysum[f, r, c] + yb[c][f]
+        return unused
+
+    lax.fori_loop(0, CW, pair, 0)
+    flux_x = [face_flux([carry[i, c] for i in range(11)], [xghost[1, i, c] for i in range(11)]) for c in range(2)]
+    finish(FW, [[carry[11 + f, c] for f in range(NF)] for c in range(2)], flux_x)
+    for c in range(2):
+        for f in range(NF):
+            xsum[1, f, c] = xsum[1, f, c] + flux_x[c][f]
 
     odd = (lane & 1) == 1
     odd_z = (lane & 16) == 16
@@ -474,14 +563,18 @@
         xedge_ref[pl.ds(f * 64 + ZC, ZC), :] = 0.5 * flux_x[f]
 
 
-def apply_kernel(count, box_ref, flag_ref, slot_ref, result_ref, base_ref, yedge_ref, zedge_ref, xedge_ref, out_ref):
+def apply_kernel(count, slot_ref, result_ref, base_ref, yedge_ref, zedge_ref, xedge_ref, out_ref, zsum):
     per_device = ZC // CW * YB
     lane = lanes()
     sub = lax.broadcasted_iota(jnp.int32, (8, LN), 0)
     out_ref[...] = base_ref[...]
+    zsum[...] = jnp.zeros(zsum.shape, jnp.float32)
+
+    def place_of(row):
+        return split_box(slot_ref[4 * count + row], per_device)[1]
 
     def weight(row, face):
-        return flag_ref[row, face].astype(jnp.float32) * (time_step if face % 2 else -time_step)
+        return slot_ref[(4 + NP) * count + row * 6 + face].astype(jnp.float32) * (time_step if face % 2 else -time_step)
 
     def one(source, unused):
         before_row, own, after_row = (slot_ref[k * count + source] for k in range(3))
@@ -499,37 +592,33 @@
 
             @pl.when(row >= 0)
             def _():
-                z0, y0 = anchors(place_of(box_ref, row, per_device))
+                z0, y0 = anchors(place_of(row))
                 scale = weight(row, upper)
                 inside = (lane >= y0) & (lane < y0 + CW)
                 index = unmix(y0, 82 if upper else 50)
                 plane = 0 if upper else CW - 1
-                places = [pl.ds(pl.multiple_of(f * 256 + plane * ZC + z0, 8), 8) for f in range(NF)]
-                new = []
+                new, places = [], []
                 for f in range(NF):
+                    place = pl.ds(pl.multiple_of(f * 256 + plane * ZC + z0, 8), 8)
                     edge = xedge_ref[pl.ds(pl.multiple_of(f * 64 + (1 - upper) * ZC + z0, 8), 8), :]
-                    old = out_ref[places[f], :]
+                    old = out_ref[place, :]
+                    places.append(place)
                     new.append(jnp.where(inside, old + scale * (take_lanes(tile(f), index) - edge), old))
-                for f in range(NF):
-                    out_ref[places[f], :] = new[f]
+                for place, value in zip(places, new):
+                    out_ref[place, :] = value
 
         @pl.when(own >= 0)
         def _():
-            place = place_of(box_ref, own, per_device)
-            z0, y0 = anchors(place)
+            z0, y0 = anchors(place_of(own))
             inside = (lane >= y0) & (lane < y0 + CW)
-            below = (z0 - 1) & (ZC - 1)
-            above = (z0 + CW) & (ZC - 1)
-            for upper, target, face in ((0, below, z0), (1, above, above)):
-                scale = weight(own, 2 + upper)
+            block = z0 >> 3
+            for upper, target, face in ((0, (block - 1) & 3, block), (1, (block + 1) & 3, (block + 1) & 3)):
+                scale = jnp.where(inside, weight(own, 2 + upper), 0.0)
                 index = unmix(y0, 114 if upper else 18)
-                new = []
                 for f in range(NF):
-                    edge = zedge_ref[pl.ds(pl.multiple_of(f * 32 + face, 8), 8), :]
-                    old = out_ref[pl.ds(f * 256 + target, 8, stride=ZC), :]
-                    new.append(jnp.where(inside, old + scale * (take_lanes(tile(f), index) - edge), old))
-                for f in range(NF):
-                    out_ref[pl.ds(f * 256 + target, 8, stride=ZC), :] = new[f]
+                    edge = zedge_ref[pl.ds(pl.multiple_of(f * 32 + face * 8, 8), 8), :]
+                    part = jnp.where(inside, take_lanes(tile(f), index) - edge, 0.0)
+                    zsum[f, upper, target] = zsum[f, upper, target] + scale * part
             before = lane == ((y0 - 1) & (LN - 1))
             after = lane == ((y0 + CW) & (LN - 1))
             part = (sub & 3) * 32 + (sub >> 2)
@@ -537,18 +626,25 @@
             index = jnp.where(inside, part + 2 * ((lane - y0) & 7), faces)
             scale = jnp.where(before, weight(own, 4), jnp.where(after, weight(own, 5), 0.0))
             for f in range(NF):
-                places = [pl.ds(pl.multiple_of(f * 256 + x * ZC + z0, 8), 8) for x in range(CW)]
-                new = []
+                new, places = [], []
                 for x in range(CW):
+                    place = pl.ds(pl.multiple_of(f * 256 + x * ZC + z0, 8), 8)
                     line = jnp.broadcast_to(result_ref[pl.ds(row0 + f * 8 + x, 1), :], (8, LN))
                     got = take_lanes(line, index)
-                    new.append(jnp.where(inside, got, out_ref[places[x], :] + scale * (got - yedge_ref[places[x], :])))
-                for x in range(CW):
-                    out_ref[places[x], :] = new[x]
+                    places.append(place)
+                    new.append(jnp.where(inside, got, out_ref[place, :] + scale * (got - yedge_ref[place, :])))
+                for place, value in zip(places, new):
+                    out_ref[place, :] = value
 
         return unused
 
     lax.fori_loop(0, count, one, 0)
+    for f in range(NF):
+        for x in range(CW):
+            for block in range(ZC // CW):
+                for upper in range(2):
+                    row = pl.ds(f * 256 + x * ZC + block * 8 + (0 if upper else 7), 1)
+                    out_ref[row, :] = out_ref[row, :] + zsum[f, upper, block, x : x + 1]
 
 
 def local(coarse_state, fine_state, patch_box, face_flags):
@@ -599,13 +695,26 @@
     ring = [(i, (i + 1) % count) for i in range(count)]
     low = lax.ppermute(last, "box", ring)
     high = lax.ppermute(first, "box", [(b, a) for a, b in ring])
-    given = call(
-        spread_kernel, shaped(NF, FW, 2, NP, LN), [hbm], vmem, 1000000, 4000000, (pltpu.SemaphoreType.DMA((2 * NP,)),)
+    middle, cells = call(
+        interior_kernel,
+        (
+            shaped(NF, FW + 1, 2, NP, LN),
+            shaped(9, FW, 2, NP, LN),
+        ),
+        [hbm],
+        (vmem, vmem),
+        10000000,
+        4000000,
+        (
+            pltpu.VMEM((NF, FW, 2, NP, LN), f32),
+            pltpu.VMEM((16, 2, 8, LN), f32),
+            pltpu.SemaphoreType.DMA((2 * NP,)),
+        ),
     )(fine_state)
     outbox, state = call(
         functools.partial(fine_kernel, count),
         (shaped(count * 40, LN), shaped(NF, FW + 1, 2, NP, LN)),
-        [smem, vmem, vmem],
+        [smem] + [vmem] * 3,
         (vmem, vmem),
         20000000,
         4000000,
@@ -615,7 +724,7 @@
             pltpu.VMEM((11, CW, 8, LN), f32),
             pltpu.VMEM((11, 2, CW, 8, LN), f32),
             pltpu.VMEM((2, 11, 2, 8, LN), f32),
-            pltpu.VMEM((NF, FW + 1, 2, 8, LN), f32),
+            pltpu.VMEM((NF, FW, 2, 8, LN), f32),
             pltpu.VMEM((16, 2, 8, LN), f32),
             pltpu.VMEM((NF, CW, 8, LN), f32),
             pltpu.VMEM((NF, CW, 2, 8, LN), f32),
@@ -623,7 +732,7 @@
             pltpu.VMEM((4 * NF, NP, LN), f32),
             pltpu.VMEM((NP * 40, LN), f32),
         ),
-    )(patch_box, arrived.reshape(count * 16, LN), given)
+    )(patch_box, arrived.reshape(count * 16, LN), middle, cells)
     returned = lax.all_to_all(outbox.reshape(count, 40, LN), "box", split_axis=0, concat_axis=0, tiled=True)
     fine_next = call(
         collect_kernel,
@@ -634,6 +743,7 @@
         4000000,
         (pltpu.SemaphoreType.DMA((2 * NP,)),),
     )(state)
+    tables = jnp.concatenate([slots, patch_box, face_flags.reshape(-1)])
     size = NF * CW * ZC
     base, yedge, zedge, xedge = call(
         coarse_kernel,
@@ -645,8 +755,14 @@
         (pltpu.VMEM((16, ZC, LN), f32),),
     )(coarse, low.reshape(NF * ZC, LN), high.reshape(NF * ZC, LN))
     coarse_next = call(
-        functools.partial(apply_kernel, count), shaped(size, LN), [smem] * 3 + [vmem] * 5, vmem, 2000000, 4000000
-    )(patch_box, face_flags, slots, returned.reshape(count * 40, LN), base, yedge, zedge, xedge)
+        functools.partial(apply_kernel, count),
+        shaped(size, LN),
+        [smem] + [vmem] * 5,
+        vmem,
+        2000000,
+        4000000,
+        (pltpu.VMEM((NF, 2, ZC // CW, CW, LN), f32),),
+    )(tables, returned.reshape(count * 40, LN), base, yedge, zedge, xedge)
     return coarse_next.reshape(coarse_state.shape), fine_next
 
 

time: 53.4 us -> 49.5 us (0.927)
  waiting for transfers between devices: 14.5 us -> 9.99 us
  local copies, waits for them, and re-layouts: 0.81 us -> 3.38 us
  Pallas kernels: 21.1 us -> 18.6 us
  other arithmetic: 0 us -> 0.76 us
    all_to_all x1, waiting for transfers between devices: 7.25 us -> 4.27 us  [local(): lax.all_to_all(packets.reshape(count, 16, LN), 'box', split_axis=0, conca...]
    pallas_call x1, Pallas kernels: 8.35 us -> 5.5 us  [local(): call(functools.partial(fine_kernel, count), (shaped(count * 40, LN), shap...]
    unnamed x15 -> x9, local copies, waits for them, and re-layouts: 0.81 us -> 3.25 us
    ppermute x1, waiting for transfers between devices: 7.29 us -> 5.72 us  [local(): low = lax.ppermute(last, 'box', ring)]
    concatenate x0 -> x1, other arithmetic: none -> 0.76 us  [local(): tables = jnp.concatenate([slots, patch_box, face_flags.reshape(-1)])]
    pallas_call x2, Pallas kernels: 5.83 us -> 6.57 us  [the longest x1 4.04 us: local(): call(functools.partial(apply_kernel, count), shaped(size, LN), [smem] + [...]
  transfers between devices with their start and end apart: 4 -> 4, of which waited for: 2 -> 2; matrix products, arithmetic and copies ran while one was open for 0% -> 3% of each run, Pallas kernels for 7% -> 11%
where the time goes in v2:
time: 49.5 us; the launch traced here: 49.1 us
  Pallas kernels  18.6 us (38%)
  starting transfers between devices  15.7 us (32%)
  waiting for transfers between devices  9.99 us (20%)
  local copies, waits for them, and re-layouts  3.38 us (7%)
  other arithmetic  0.76 us (2%)
  between operations  0.72 us (1%)
    all_to_all x1, starting transfers between devices, local(): lax.all_to_all(packets.reshape(count, 16, LN), 'box', split_axis=0, conca...  7.64 us
    ppermute x1, waiting for transfers between devices, local(): low = lax.ppermute(last, 'box', ring)  5.72 us
    pallas_call x1, Pallas kernels, local(): call(functools.partial(fine_kernel, count), (shaped(count * 40, LN), shap...  5.5 us
    all_to_all x1, waiting for transfers between devices, local(): lax.all_to_all(packets.reshape(count, 16, LN), 'box', split_axis=0, conca...  4.27 us
    ppermute x1, starting transfers between devices, local(): high = lax.ppermute(first, 'box', [(b, a) for a, b in ring])  4.2 us
    pallas_call x1, Pallas kernels, local(): call(functools.partial(apply_kernel, count), shaped(size, LN), [smem] + [...  4.04 us
    pallas_call x1, Pallas kernels, local(): call(functools.partial(pack_kernel, count), (shaped(count * 16, LN), shap...  3.62 us
    all_to_all x1, starting transfers between devices, local(): lax.all_to_all(outbox.reshape(count, 40, LN), 'box', split_axis=0, concat...  3.54 us
  transfers between devices with their start and end apart: 4, of which 2 were waited for; matrix products, arithmetic and copies ran while one was open for 3% of the time, Pallas kernels for 11%

profile of v2, /device:TPU:0, one launch (start us, length us, event | category | flops | bytes accessed | tf_op | source)
XLA Modules:
  0.0 49.1 jit_solution(16941163743522972121)
XLA Ops:
  0.6 3.6 %shard_map.59 = (f32[256,128]{1,0:T(8,128)}, f32[5,32,128]{2,1,0:T(8,128)}, f32[5,32,128]{2,1,0:T(8,128)}, s32[64]{0:T(128)}, s32[18]{0:T(128)}) custom-call(s32[128]{0:T(128)} %box_ref.1, f32[5,8,32,128]{3,2,1,0:T(8,128)} %coarse_hbm.1), custom_call_target="tpu_custom_call" | custom-call | flops 1000000 | bytes 1000000 | tf_op jit(solution)/shard_map/pallas_call | solution.py:674
  4.3 7.6 %all-to-all-start = ((f32[16,16,128]{2,1,0:T(8,128)}), f32[16,16,128]{2,1,0:T(8,128)S(1)}, u32[]{:S(2)}, u32[]{:S(2)}) async-start(f32[16,16,128]{2,1,0:T(8,128)} %bitcast.15), calls=%async_computation | async-start | bytes 262144 | tf_op jit(solution)/shard_map/all_to_all | solution.py:694
  11.9 0.0 copy-start.1
  11.9 1.1 %copy-done.1 = f32[8,5,16,256]{3,2,1,0:T(8,128)S(1)} copy-done((f32[8,5,16,256]{3,2,1,0:T(8,128)S(1)}, f32[8,5,16,256]{3,2,1,0:T(8,128)}, u32[]{:S(2)}) %copy-start.1) | copy-done | bytes 655384
  13.0 2.5 %shard_map.60 = (f32[5,17,2,8,128]{4,3,2,1,0:T(8,128)S(1)}, f32[9,16,2,8,128]{4,3,2,1,0:T(8,128)S(1)}) custom-call(f32[8,5,16,256]{3,2,1,0:T(8,128)S(1)} %copy-done.1), custom_call_target="tpu_custom_call" | custom-call | flops 10000000 | bytes 4000000 | tf_op jit(solution)/shard_map/pallas_call | solution.py:698
  15.5 4.3 %all-to-all-done = f32[16,16,128]{2,1,0:T(8,128)S(1)} async-done(((f32[16,16,128]{2,1,0:T(8,128)}), f32[16,16,128]{2,1,0:T(8,128)S(1)}, u32[]{:S(2)}, u32[]{:S(2)}) %all-to-all-start) | async-done | bytes 131104 | tf_op jit(solution)/shard_map/all_to_all | solution.py:694
  19.8 0.0 copy-start.3
  19.8 0.7 %copy-done.3 = s32[128]{0:T(128)S(1)} copy-done((s32[128]{0:T(128)S(1)}, s32[128]{0:T(128)}, u32[]{:S(2)}) %copy-start.3) | copy-done | bytes 536
  20.5 0.0 copy-start
  20.5 5.5 %shard_map.61 = (f32[640,128]{1,0:T(8,128)S(1)}, f32[5,17,2,8,128]{4,3,2,1,0:T(8,128)S(1)}) custom-call(s32[128]{0:T(128)S(1)} %copy-done.3, f32[256,128]{1,0:T(8,128)S(1)} %bitcast.10, f32[5,17,2,8,128]{4,3,2,1,0:T(8,128)S(1)} %get-tuple-element.16.middle_ref, f32[9,16,2,8,128]{4,3,2,1,0:T(8,128)S(1)} %get-tuple-element.17.cells_ref), custom_call_target="tpu_custom_call" | custom-call | flops 20000000 | bytes 4000000 | tf_op jit(solution)/shard_map/pallas_call | solution.py:714
  26.0 0.0 copy-start.2
  26.0 0.7 %copy-done.2 = f32[640,128]{1,0:T(8,128)} copy-done((f32[640,128]{1,0:T(8,128)}, f32[640,128]{1,0:T(8,128)S(1)}, u32[]{:S(2)}) %copy-start.2) | copy-done | bytes 327704
  26.7 3.5 %all-to-all-start.1 = ((f32[16,40,128]{2,1,0:T(8,128)}), f32[16,40,128]{2,1,0:T(8,128)S(1)}, u32[]{:S(2)}, u32[]{:S(2)}) async-start(f32[16,40,128]{2,1,0:T(8,128)} %bitcast.11), calls=%async_computation.1 | async-start | bytes 655360 | tf_op jit(solution)/shard_map/all_to_all | solution.py:736
  30.2 0.3 collective-permute-start
  30.5 4.2 %collective-permute-start.1 = (f32[5,32,128]{2,1,0:T(8,128)}, f32[5,32,128]{2,1,0:T(8,128)S(1)}, u32[]{:S(2)}, u32[]{:S(2)}) collective-permute-start(f32[5,32,128]{2,1,0:T(8,128)} %get-tuple-element.20), channel_id=1, source_target_pairs={{1,0},{2,1},{3,2},{4,3},{5,4},{6,5},{7,6},{8,7},{9,8},{10,9},{11,1... | collective-permute-start | bytes 245768 | tf_op jit(solution)/shard_map/ppermute | solution.py:697
  34.7 0.8 %copy.6 = s32[128,6]{1,0:T(8,128)S(1)} copy(s32[128,6]{0,1:T(8,128)} %param.7) | data formatting | bytes 6144 | tf_op args[3]
  35.5 0.1 reshape.31
  35.7 0.8 %pad_add_fusion.slot_ref = s32[960]{0:T(1024)S(1)} fusion(s32[768]{0:T(1024)S(1)} %reshape.31, s32[128]{0:T(128)} %box_ref.1, s32[64]{0:T(128)} %get-tuple-element.14), kind=kLoop, calls=%fused_computation | loop fusion | flops 1920 | bytes 7680 | tf_op jit(solution)/shard_map/concatenate | solution.py:746
  36.4 5.7 %collective-permute-done = f32[5,32,128]{2,1,0:T(8,128)S(1)} collective-permute-done((f32[5,32,128]{2,1,0:T(8,128)}, f32[5,32,128]{2,1,0:T(8,128)S(1)}, u32[]{:S(2)}, u32[]{:S(2)}) %collective-permute-start) | collective-permute-done | bytes 81952 | tf_op jit(solution)/shard_map/ppermute | solution.py:696
  42.2 0.0 collective-permute-done.1
  42.2 0.0 copy-done
  42.2 1.9 %shard_map.62 = (f32[1280,128]{1,0:T(8,128)S(1)}, f32[1280,128]{1,0:T(8,128)S(1)}, f32[160,128]{1,0:T(8,128)S(1)}, f32[320,128]{1,0:T(8,128)S(1)}) custom-call(f32[1280,128]{1,0:T(8,128)S(1)} %bitcast.8, f32[160,128]{1,0:T(8,128)S(1)} %bitcast.12, f32[160,128]{1,0:T(8,128)S(1)} %bitcast.13), custom_call_target="tpu_custom_call" | custom-call | flops 10000000 | bytes 4000000 | tf_op jit(solution)/shard_map/pallas_call | solution.py:748
  44.1 1.0 %shard_map.64 = f32[8,5,16,256]{3,2,1,0:T(8,128)} custom-call(f32[5,17,2,8,128]{4,3,2,1,0:T(8,128)S(1)} %get-tuple-element.25.state_ref), custom_call_target="tpu_custom_call" | custom-call | flops 1000000 | bytes 4000000 | tf_op jit(solution)/shard_map/pallas_call | solution.py:737
  45.1 0.0 all-to-all-done.1
  45.1 4.0 %shard_map.63 = f32[1280,128]{1,0:T(8,128)} custom-call(s32[960]{0:T(1024)S(1)} %pad_add_fusion.slot_ref, f32[640,128]{1,0:T(8,128)S(1)} %bitcast.9, f32[1280,128]{1,0:T(8,128)S(1)} %get-tuple-element.21.base_ref, f32[1280,128]{1,0:T(8,128)S(1)} %get-tuple-element.22.yedge_ref, f32[160,128]{1,0:T(8,128)S(1)} %get-tuple-element.23.zedge_ref, ...), custom_call_target="tpu_custom_call" | custom-call | flops 2000000 | bytes 4000000 | tf_op jit(solution)/shard_map/pallas_call | solution.py:757
Async XLA Ops:
  4.3 15.6 %all-to-all-start = ((f32[16,16,128]{2,1,0:T(8,128)}), f32[16,16,128]{2,1,0:T(8,128)S(1)}, u32[]{:S(2)}, u32[]{:S(2)}) async-start(f32[16,16,128]{2,1,0:T(8,128)} %bitcast.15), calls=%async_computation | async-start | bytes 262144 | tf_op jit(solution)/shard_map/all_to_all | solution.py:694
  11.9 1.1 %copy-start.1 = (f32[8,5,16,256]{3,2,1,0:T(8,128)S(1)}, f32[8,5,16,256]{3,2,1,0:T(8,128)}, u32[]{:S(2)}) copy-start(f32[8,5,16,256]{3,2,1,0:T(8,128)} %fine_ref.1) | copy-start | bytes 1966084
  19.8 0.7 %copy-start.3 = (s32[128]{0:T(128)S(1)}, s32[128]{0:T(128)}, u32[]{:S(2)}) copy-start(s32[128]{0:T(128)} %box_ref.1) | copy-start | bytes 1540
  20.5 21.7 %copy-start = (f32[5,8,32,128]{3,2,1,0:T(8,128)S(1)}, f32[5,8,32,128]{3,2,1,0:T(8,128)}, u32[]{:S(2)}) copy-start(f32[5,8,32,128]{3,2,1,0:T(8,128)} %coarse_hbm.1) | copy-start | bytes 1966084
  26.0 0.7 %copy-start.2 = (f32[640,128]{1,0:T(8,128)}, f32[640,128]{1,0:T(8,128)S(1)}, u32[]{:S(2)}) copy-start(f32[640,128]{1,0:T(8,128)S(1)} %get-tuple-element.18) | copy-start | bytes 983044
  26.7 18.4 %all-to-all-start.1 = ((f32[16,40,128]{2,1,0:T(8,128)}), f32[16,40,128]{2,1,0:T(8,128)S(1)}, u32[]{:S(2)}, u32[]{:S(2)}) async-start(f32[16,40,128]{2,1,0:T(8,128)} %bitcast.11), calls=%async_computation.1 | async-start | bytes 655360 | tf_op jit(solution)/shard_map/all_to_all | solution.py:736
  30.2 11.9 %collective-permute-start = (f32[5,32,128]{2,1,0:T(8,128)}, f32[5,32,128]{2,1,0:T(8,128)S(1)}, u32[]{:S(2)}, u32[]{:S(2)}) collective-permute-start(f32[5,32,128]{2,1,0:T(8,128)} %get-tuple-element.19), channel_id=1, source_target_pairs={{0,1},{1,2},{2,3},{3,4},{4,5},{5,6},{6,7},{7,8},{8,9},{9,10},{10,1... | collective-permute-start | bytes 245768 | tf_op jit(solution)/shard_map/ppermute | solution.py:696
  30.5 11.6 %collective-permute-start.1 = (f32[5,32,128]{2,1,0:T(8,128)}, f32[5,32,128]{2,1,0:T(8,128)S(1)}, u32[]{:S(2)}, u32[]{:S(2)}) collective-permute-start(f32[5,32,128]{2,1,0:T(8,128)} %get-tuple-element.20), channel_id=1, source_target_pairs={{1,0},{2,1},{3,2},{4,3},{5,4},{6,5},{7,6},{8,7},{9,8},{10,9},{11,1... | collective-permute-start | bytes 245768 | tf_op jit(solution)/shard_map/ppermute | solution.py:697

commit v3 on v2

--- a/solution.py
+++ b/solution.py
@@ -123,7 +123,7 @@
         copy.start()
     numbers.wait()
     fill_slots(box_ref, slot_ref, own_ref, me, count, per_device)
-    for copy in copies:
+    for copy in copies[:2]:
         copy.wait()
     spot = jnp.where((lane >= 16) & (lane < 24), lane - 16, jnp.where((lane >= 25) & (lane < 33), lane - 25, -1))
 
@@ -146,6 +146,8 @@
         return unused
 
     lax.fori_loop(0, count // 4, edges, 0)
+    for copy in copies[2:]:
+        copy.wait()
 
     def faces(pair, unused):
         for i in range(2):
@@ -380,6 +382,14 @@
             xsum[side, f] = flux_x[f]
             middle[f, plane] = middle[f, plane] + (-step if side else step) * flux_x[f]
 
+    def raw_of(cells, prims, m):
+        return cells + [prims[0][m], prims[1], prims[2]]
+
+    def side_of_raw(raw, m):
+        speeds = [None] * 4
+        speeds[m] = raw[5]
+        return side_of_face(raw[:NF], (speeds, raw[6], raw[7], raw[4] + raw[6]), m)
+
     def finish(plane, part, flux):
         for c in range(2):
             for f in range(NF):
@@ -416,11 +426,13 @@
                         for f in range(NF):
                             xsum[0, f, c] = xsum[0, f, c] + flux_x[c][f]
 
-            here = [side_of_face(cells[c], prims[c], 3) for c in range(2)]
-            turned = [[roll_to(v, 16) for v in here[c]] for c in range(2)]
+            raw = [raw_of(cells[c], prims[c], 3) for c in range(2)]
+            here = [side_of_raw(raw[c], 3) for c in range(2)]
+            turned = [[roll_to(v, 16) for v in raw[c]] for c in range(2)]
+            left = side_of_raw(turned[0], 3)
             left = [
-                [jnp.where(low16, zg[i], turned[0][i]) for i in range(11)],
-                [jnp.where(low16, turned[0][i], turned[1][i]) for i in range(11)],
+                [jnp.where(low16, zg[i], left[i]) for i in range(11)],
+                side_of_raw([jnp.where(low16, a, b) for a, b in zip(*turned)], 3),
             ]
             lower = [face_flux(left[c], here[c]) for c in range(2)]
             last = face_flux(here[1], zg)
@@ -433,8 +445,10 @@
                 zb[f] = edge if half == 0 else zb[f] + edge
             for c in range(2):
                 yg = [yghost[i, c, r] for i in range(11)]
-                here = side_of_face(cells[c], prims[c], 2)
-                left = [jnp.where(first_y, yg[i], roll_to(here[i], 1)) for i in range(11)]
+                raw = raw_of(cells[c], prims[c], 2)
+                here = side_of_raw(raw, 2)
+                left = side_of_raw([roll_to(v, 1) for v in raw], 2)
+                left = [jnp.where(first_y, yg[i], left[i]) for i in range(11)]
                 lower_y = face_flux(left, here)
                 last_flux = face_flux(here, yg)
                 for f in range(NF):
@@ -461,6 +475,8 @@
     odd = (lane & 1) == 1
     odd_z = (lane & 16) == 16
     outer = (place_y == 0) | (place_y == 15)
+    middle_y = (place_y >= 2) & (place_y < 10)
+    z_ends = (lane < 16) | (lane >= 112)
 
     def shifted(values, shift):
         return [roll_to(v, shift) for v in values]
@@ -486,11 +502,12 @@
         fluxes = [
             jnp.where(outer, v[0][r], jnp.where(place_y < 8, turned[0][r], turned[1][r])) for r in range(CW)
         ]
+        v = [zsum[f, r] for r in range(CW)]
+        v = added(v, shifted(v, -1))
+        v = [jnp.where(odd, b, a) for a, b in zip(shifted(v, 2), shifted(v, -5))]
+        fluxes = [jnp.where(middle_y, jnp.where(z_ends, v[r], 0.0), fluxes[r]) for r in range(CW)]
         fluxes = added(fluxes, shifted(fluxes, 16))
-        ends = dense([zsum[f, r] for r in range(CW)])
         for low, part in (
-            (18, shifted(ends, 18)),
-            (114, shifted(ends, 2)),
             (50, [roll_to(xpool[f * 4 + r // 4], 50 - r % 4 * 32) for r in range(CW)]),
             (82, [roll_to(xpool[f * 4 + 2 + r // 4], 82 - r % 4 * 32) for r in range(CW)]),
         ):
@@ -563,7 +580,7 @@
         xedge_ref[pl.ds(f * 64 + ZC, ZC), :] = 0.5 * flux_x[f]
 
 
-def apply_kernel(count, slot_ref, result_ref, base_ref, yedge_ref, zedge_ref, xedge_ref, out_ref, zsum):
+def apply_kernel(count, slot_ref, result_ref, base_ref, yedge_ref, zedge_ref, xedge_ref, out_hbm, zsum, out_ref, semaphores):
     per_device = ZC // CW * YB
     lane = lanes()
     sub = lax.broadcasted_iota(jnp.int32, (8, LN), 0)
@@ -639,12 +656,18 @@
         return unused
 
     lax.fori_loop(0, count, one, 0)
+    copies = []
     for f in range(NF):
         for x in range(CW):
             for block in range(ZC // CW):
                 for upper in range(2):
                     row = pl.ds(f * 256 + x * ZC + block * 8 + (0 if upper else 7), 1)
                     out_ref[row, :] = out_ref[row, :] + zsum[f, upper, block, x : x + 1]
+        field = pl.ds(f * 256, 256)
+        copies.append(pltpu.make_async_copy(out_ref.at[field, :], out_hbm.at[field, :], semaphores.at[f]))
+        copies[f].start()
+    for copy in copies:
+        copy.wait()
 
 
 def local(coarse_state, fine_state, patch_box, face_flags):
@@ -758,10 +781,14 @@
         functools.partial(apply_kernel, count),
         shaped(size, LN),
         [smem] + [vmem] * 5,
-        vmem,
+        anywhere,
         2000000,
         4000000,
-        (pltpu.VMEM((NF, 2, ZC // CW, CW, LN), f32),),
+        (
+            pltpu.VMEM((NF, 2, ZC // CW, CW, LN), f32),
+            pltpu.VMEM((size, LN), f32),
+            pltpu.SemaphoreType.DMA((NF,)),
+        ),
     )(tables, returned.reshape(count * 40, LN), base, yedge, zedge, xedge)
     return coarse_next.reshape(coarse_state.shape), fine_next
 

time: 49.5 us -> 48.8 us (0.986)
  Pallas kernels: 18.6 us -> 17.8 us
    pallas_call x1, Pallas kernels: 5.5 us -> 4.85 us  [local(): call(functools.partial(fine_kernel, count), (shaped(count * 40, LN), shap...]
where the time goes in v3:
time: 48.8 us; the launch traced here: 48.4 us
  Pallas kernels  17.8 us (36%)
  starting transfers between devices  15.7 us (32%)
  waiting for transfers between devices  9.99 us (20%)
  local copies, waits for them, and re-layouts  3.38 us (7%)
  other arithmetic  0.76 us (2%)
  between operations  0.72 us (1%)
    all_to_all x1, starting transfers between devices, local(): lax.all_to_all(packets.reshape(count, 16, LN), 'box', split_axis=0, conca...  7.64 us
    ppermute x1, waiting for transfers between devices, local(): low = lax.ppermute(last, 'box', ring)  5.72 us
    pallas_call x1, Pallas kernels, local(): call(functools.partial(fine_kernel, count), (shaped(count * 40, LN), shap...  4.85 us
    all_to_all x1, waiting for transfers between devices, local(): lax.all_to_all(packets.reshape(count, 16, LN), 'box', split_axis=0, conca...  4.27 us
    ppermute x1, starting transfers between devices, local(): high = lax.ppermute(first, 'box', [(b, a) for a, b in ring])  4.2 us
    pallas_call x1, Pallas kernels, local(): call(functools.partial(apply_kernel, count), shaped(size, LN), [smem] + [...  3.93 us
    pallas_call x1, Pallas kernels, local(): call(functools.partial(pack_kernel, count), (shaped(count * 16, LN), shap...  3.62 us
    all_to_all x1, starting transfers between devices, local(): lax.all_to_all(outbox.reshape(count, 40, LN), 'box', split_axis=0, concat...  3.54 us
  transfers between devices with their start and end apart: 4, of which 2 were waited for; matrix products, arithmetic and copies ran while one was open for 3% of the time, Pallas kernels for 11%

profile of v3, /device:TPU:0, one launch (start us, length us, event | category | flops | bytes accessed | tf_op | source)
XLA Modules:
  0.0 48.4 jit_solution(4816976737142981130)
XLA Ops:
  0.6 3.6 %shard_map.59 = (f32[256,128]{1,0:T(8,128)}, f32[5,32,128]{2,1,0:T(8,128)}, f32[5,32,128]{2,1,0:T(8,128)}, s32[64]{0:T(128)}, s32[18]{0:T(128)}) custom-call(s32[128]{0:T(128)} %box_ref.1, f32[5,8,32,128]{3,2,1,0:T(8,128)} %coarse_hbm.1), custom_call_target="tpu_custom_call" | custom-call | flops 1000000 | bytes 1000000 | tf_op jit(solution)/shard_map/pallas_call | solution.py:697
  4.3 7.6 %all-to-all-start = ((f32[16,16,128]{2,1,0:T(8,128)}), f32[16,16,128]{2,1,0:T(8,128)S(1)}, u32[]{:S(2)}, u32[]{:S(2)}) async-start(f32[16,16,128]{2,1,0:T(8,128)} %bitcast.15), calls=%async_computation | async-start | bytes 262144 | tf_op jit(solution)/shard_map/all_to_all | solution.py:717
  11.9 0.0 copy-start.1
  11.9 1.1 %copy-done.1 = f32[8,5,16,256]{3,2,1,0:T(8,128)S(1)} copy-done((f32[8,5,16,256]{3,2,1,0:T(8,128)S(1)}, f32[8,5,16,256]{3,2,1,0:T(8,128)}, u32[]{:S(2)}) %copy-start.1) | copy-done | bytes 655384
  13.0 2.5 %shard_map.60 = (f32[5,17,2,8,128]{4,3,2,1,0:T(8,128)S(1)}, f32[9,16,2,8,128]{4,3,2,1,0:T(8,128)S(1)}) custom-call(f32[8,5,16,256]{3,2,1,0:T(8,128)S(1)} %copy-done.1), custom_call_target="tpu_custom_call" | custom-call | flops 10000000 | bytes 4000000 | tf_op jit(solution)/shard_map/pallas_call | solution.py:721
  15.5 4.3 %all-to-all-done = f32[16,16,128]{2,1,0:T(8,128)S(1)} async-done(((f32[16,16,128]{2,1,0:T(8,128)}), f32[16,16,128]{2,1,0:T(8,128)S(1)}, u32[]{:S(2)}, u32[]{:S(2)}) %all-to-all-start) | async-done | bytes 131104 | tf_op jit(solution)/shard_map/all_to_all | solution.py:717
  19.8 0.0 copy-start.3
  19.8 0.7 %copy-done.3 = s32[128]{0:T(128)S(1)} copy-done((s32[128]{0:T(128)S(1)}, s32[128]{0:T(128)}, u32[]{:S(2)}) %copy-start.3) | copy-done | bytes 536
  20.5 0.0 copy-start
  20.5 4.8 %shard_map.61 = (f32[640,128]{1,0:T(8,128)S(1)}, f32[5,17,2,8,128]{4,3,2,1,0:T(8,128)S(1)}) custom-call(s32[128]{0:T(128)S(1)} %copy-done.3, f32[256,128]{1,0:T(8,128)S(1)} %bitcast.10, f32[5,17,2,8,128]{4,3,2,1,0:T(8,128)S(1)} %get-tuple-element.16.middle_ref, f32[9,16,2,8,128]{4,3,2,1,0:T(8,128)S(1)} %get-tuple-element.17.cells_ref), custom_call_target="tpu_custom_call" | custom-call | flops 20000000 | bytes 4000000 | tf_op jit(solution)/shard_map/pallas_call | solution.py:737
  25.3 0.0 copy-start.2
  25.3 0.7 %copy-done.2 = f32[640,128]{1,0:T(8,128)} copy-done((f32[640,128]{1,0:T(8,128)}, f32[640,128]{1,0:T(8,128)S(1)}, u32[]{:S(2)}) %copy-start.2) | copy-done | bytes 327704
  26.1 3.5 %all-to-all-start.1 = ((f32[16,40,128]{2,1,0:T(8,128)}), f32[16,40,128]{2,1,0:T(8,128)S(1)}, u32[]{:S(2)}, u32[]{:S(2)}) async-start(f32[16,40,128]{2,1,0:T(8,128)} %bitcast.11), calls=%async_computation.1 | async-start | bytes 655360 | tf_op jit(solution)/shard_map/all_to_all | solution.py:759
  29.6 0.3 collective-permute-start
  29.9 4.2 %collective-permute-start.1 = (f32[5,32,128]{2,1,0:T(8,128)}, f32[5,32,128]{2,1,0:T(8,128)S(1)}, u32[]{:S(2)}, u32[]{:S(2)}) collective-permute-start(f32[5,32,128]{2,1,0:T(8,128)} %get-tuple-element.20), channel_id=1, source_target_pairs={{1,0},{2,1},{3,2},{4,3},{5,4},{6,5},{7,6},{8,7},{9,8},{10,9},{11,1... | collective-permute-start | bytes 245768 | tf_op jit(solution)/shard_map/ppermute | solution.py:720
  34.1 0.8 %copy.6 = s32[128,6]{1,0:T(8,128)S(1)} copy(s32[128,6]{0,1:T(8,128)} %param.7) | data formatting | bytes 6144 | tf_op args[3]
  34.9 0.1 reshape.31
  35.0 0.8 %pad_add_fusion.slot_ref = s32[960]{0:T(1024)S(1)} fusion(s32[768]{0:T(1024)S(1)} %reshape.31, s32[128]{0:T(128)} %box_ref.1, s32[64]{0:T(128)} %get-tuple-element.14), kind=kLoop, calls=%fused_computation | loop fusion | flops 1920 | bytes 7680 | tf_op jit(solution)/shard_map/concatenate | solution.py:769
  35.8 5.7 %collective-permute-done = f32[5,32,128]{2,1,0:T(8,128)S(1)} collective-permute-done((f32[5,32,128]{2,1,0:T(8,128)}, f32[5,32,128]{2,1,0:T(8,128)S(1)}, u32[]{:S(2)}, u32[]{:S(2)}) %collective-permute-start) | collective-permute-done | bytes 81952 | tf_op jit(solution)/shard_map/ppermute | solution.py:719
  41.5 0.0 collective-permute-done.1
  41.5 0.0 copy-done
  41.5 1.9 %shard_map.62 = (f32[1280,128]{1,0:T(8,128)S(1)}, f32[1280,128]{1,0:T(8,128)S(1)}, f32[160,128]{1,0:T(8,128)S(1)}, f32[320,128]{1,0:T(8,128)S(1)}) custom-call(f32[1280,128]{1,0:T(8,128)S(1)} %bitcast.8, f32[160,128]{1,0:T(8,128)S(1)} %bitcast.12, f32[160,128]{1,0:T(8,128)S(1)} %bitcast.13), custom_call_target="tpu_custom_call" | custom-call | flops 10000000 | bytes 4000000 | tf_op jit(solution)/shard_map/pallas_call | solution.py:771
  43.4 1.0 %shard_map.64 = f32[8,5,16,256]{3,2,1,0:T(8,128)} custom-call(f32[5,17,2,8,128]{4,3,2,1,0:T(8,128)S(1)} %get-tuple-element.25.state_ref), custom_call_target="tpu_custom_call" | custom-call | flops 1000000 | bytes 4000000 | tf_op jit(solution)/shard_map/pallas_call | solution.py:760
  44.4 0.0 all-to-all-done.1
  44.4 3.9 %shard_map.63 = f32[1280,128]{1,0:T(8,128)} custom-call(s32[960]{0:T(1024)S(1)} %pad_add_fusion.slot_ref, f32[640,128]{1,0:T(8,128)S(1)} %bitcast.9, f32[1280,128]{1,0:T(8,128)S(1)} %get-tuple-element.21.base_ref, f32[1280,128]{1,0:T(8,128)S(1)} %get-tuple-element.22.yedge_ref, f32[160,128]{1,0:T(8,128)S(1)} %get-tuple-element.23.zedge_ref, ...), custom_call_target="tpu_custom_call" | custom-call | flops 2000000 | bytes 4000000 | tf_op jit(solution)/shard_map/pallas_call | solution.py:780
Async XLA Ops:
  4.3 15.6 %all-to-all-start = ((f32[16,16,128]{2,1,0:T(8,128)}), f32[16,16,128]{2,1,0:T(8,128)S(1)}, u32[]{:S(2)}, u32[]{:S(2)}) async-start(f32[16,16,128]{2,1,0:T(8,128)} %bitcast.15), calls=%async_computation | async-start | bytes 262144 | tf_op jit(solution)/shard_map/all_to_all | solution.py:717
  11.9 1.1 %copy-start.1 = (f32[8,5,16,256]{3,2,1,0:T(8,128)S(1)}, f32[8,5,16,256]{3,2,1,0:T(8,128)}, u32[]{:S(2)}) copy-start(f32[8,5,16,256]{3,2,1,0:T(8,128)} %fine_ref.1) | copy-start | bytes 1966084
  19.8 0.7 %copy-start.3 = (s32[128]{0:T(128)S(1)}, s32[128]{0:T(128)}, u32[]{:S(2)}) copy-start(s32[128]{0:T(128)} %box_ref.1) | copy-start | bytes 1540
  20.5 21.1 %copy-start = (f32[5,8,32,128]{3,2,1,0:T(8,128)S(1)}, f32[5,8,32,128]{3,2,1,0:T(8,128)}, u32[]{:S(2)}) copy-start(f32[5,8,32,128]{3,2,1,0:T(8,128)} %coarse_hbm.1) | copy-start | bytes 1966084
  25.3 0.7 %copy-start.2 = (f32[640,128]{1,0:T(8,128)}, f32[640,128]{1,0:T(8,128)S(1)}, u32[]{:S(2)}) copy-start(f32[640,128]{1,0:T(8,128)S(1)} %get-tuple-element.18) | copy-start | bytes 983044
  26.1 18.4 %all-to-all-start.1 = ((f32[16,40,128]{2,1,0:T(8,128)}), f32[16,40,128]{2,1,0:T(8,128)S(1)}, u32[]{:S(2)}, u32[]{:S(2)}) async-start(f32[16,40,128]{2,1,0:T(8,128)} %bitcast.11), calls=%async_computation.1 | async-start | bytes 655360 | tf_op jit(solution)/shard_map/all_to_all | solution.py:759
  29.6 11.9 %collective-permute-start = (f32[5,32,128]{2,1,0:T(8,128)}, f32[5,32,128]{2,1,0:T(8,128)S(1)}, u32[]{:S(2)}, u32[]{:S(2)}) collective-permute-start(f32[5,32,128]{2,1,0:T(8,128)} %get-tuple-element.19), channel_id=1, source_target_pairs={{0,1},{1,2},{2,3},{3,4},{4,5},{5,6},{6,7},{7,8},{8,9},{9,10},{10,1... | collective-permute-start | bytes 245768 | tf_op jit(solution)/shard_map/ppermute | solution.py:719
  29.9 11.6 %collective-permute-start.1 = (f32[5,32,128]{2,1,0:T(8,128)}, f32[5,32,128]{2,1,0:T(8,128)S(1)}, u32[]{:S(2)}, u32[]{:S(2)}) collective-permute-start(f32[5,32,128]{2,1,0:T(8,128)} %get-tuple-element.20), channel_id=1, source_target_pairs={{1,0},{2,1},{3,2},{4,3},{5,4},{6,5},{7,6},{8,7},{9,8},{10,9},{11,1... | collective-permute-start | bytes 245768 | tf_op jit(solution)/shard_map/ppermute | solution.py:720

commit v4 on v3

--- a/solution.py
+++ b/solution.py
@@ -107,7 +107,7 @@
     return (place >> 4) * CW, (place & (YB - 1)) * CW
 
 
-def pack_kernel(count, box_hbm, coarse_hbm, out_ref, first_ref, last_ref, slot_ref, own_ref, box_ref, turned, semaphores):
+def pack_kernel(count, box_hbm, coarse_hbm, out_ref, first_ref, last_ref, slot_ref, own_ref, box_ref, turned, beside, semaphores):
     me = lax.axis_index("box")
     per_device = ZC // CW * YB
     lane = lanes()
@@ -125,7 +125,6 @@
     fill_slots(box_ref, slot_ref, own_ref, me, count, per_device)
     for copy in copies[:2]:
         copy.wait()
-    spot = jnp.where((lane >= 16) & (lane < 24), lane - 16, jnp.where((lane >= 25) & (lane < 33), lane - 25, -1))
 
     def edges(block, unused):
         for i in range(4):
@@ -149,23 +148,37 @@
     for copy in copies[2:]:
         copy.wait()
 
+    residue = lane & (CW - 1)
+
+    def columns(block, unused):
+        for f in range(NF):
+            moved = [roll_to(turned[f, block * CW + k], k + 1) for k in range(CW)]
+            low = high = moved[0]
+            for k in range(1, CW):
+                low = jnp.where(residue == k, moved[k], low)
+                high = jnp.where(residue == (k + 1) % CW, moved[k], high)
+            beside[0, f, block] = low
+            beside[1, f, block] = high
+        return unused
+
+    lax.fori_loop(0, ZC // CW, columns, 0)
+
     def faces(pair, unused):
         for i in range(2):
             own = own_ref[1 + jnp.minimum(2 * pair + i, used - 1)]
             row0 = pl.multiple_of(own // NP * 16, 16)
             z0, y0 = anchors(place_of(box_ref, own, per_device))
+            block = z0 >> 3
             below = (z0 - 1) & (ZC - 1)
             above = (z0 + CW) & (ZC - 1)
+            inside = (lane >= y0) & (lane < y0 + CW)
             sides = [None, None]
-            pieces = []
-            for f in range(NF):
-                piece = jnp.where(lane < 8, roll_to(turned[f, below], -y0), roll_to(turned[f, above], 8 - y0))
-                for k in range(CW):
-                    piece = jnp.where(spot == k, roll_to(turned[f, z0 + k], 17 + k - y0), piece)
-                pieces.append(piece)
             for f in range(NF):
                 tile, base = SIDE[f]
-                piece = roll_to(pieces[f], base)
+                low = roll_to(turned[f, below], base - y0)
+                high = roll_to(turned[f, above], base + 8 - y0)
+                both = roll_to(jnp.where(inside, beside[0, f, block], beside[1, f, block]), base + 16 - y0)
+                piece = jnp.where(lane < base + 8, low, jnp.where(lane < base + 16, high, both))
                 sides[tile] = piece if base == 0 else jnp.where(lane >= base, piece, sides[tile])
             pltpu.store(out_ref.at[pl.ds(row0, 8), :], sides[0], mask=lane < 99)
             pltpu.store(out_ref.at[pl.ds(row0 + 8, 8), :], sides[1], mask=lane < 66)
@@ -710,6 +723,7 @@
         (
             pltpu.SMEM((count * NP,), jnp.int32),
             pltpu.VMEM((NF, ZC, CW, LN), f32),
+            pltpu.VMEM((2, NF, ZC // CW, CW, LN), f32),
             pltpu.SemaphoreType.DMA((3 + CW,)),
         ),
         limit=63,

time: 48.8 us -> 48.7 us (level)
  no operation moved by 1% of the time
where the time goes in v4:
time: 48.7 us; the launch traced here: 48.2 us
  Pallas kernels  17.8 us (37%)
  starting transfers between devices  15.6 us (32%)
  waiting for transfers between devices  9.99 us (21%)
  local copies, waits for them, and re-layouts  3.38 us (7%)
  other arithmetic  0.76 us (2%)
  between operations  0.72 us (1%)
    all_to_all x1, starting transfers between devices, local(): lax.all_to_all(packets.reshape(count, 16, LN), 'box', split_axis=0, conca...  7.54 us
    ppermute x1, waiting for transfers between devices, local(): low = lax.ppermute(last, 'box', ring)  5.72 us
    pallas_call x1, Pallas kernels, local(): call(functools.partial(fine_kernel, count), (shaped(count * 40, LN), shap...  4.85 us
    all_to_all x1, waiting for transfers between devices, local(): lax.all_to_all(packets.reshape(count, 16, LN), 'box', split_axis=0, conca...  4.27 us
    ppermute x1, starting transfers between devices, local(): high = lax.ppermute(first, 'box', [(b, a) for a, b in ring])  4.2 us
    pallas_call x1, Pallas kernels, local(): call(functools.partial(apply_kernel, count), shaped(size, LN), [smem] + [...  3.93 us
    pallas_call x1, Pallas kernels, local(): call(functools.partial(pack_kernel, count), (shaped(count * 16, LN), shap...  3.62 us
    all_to_all x1, starting transfers between devices, local(): lax.all_to_all(outbox.reshape(count, 40, LN), 'box', split_axis=0, concat...  3.54 us
  transfers between devices with their start and end apart: 4, of which 2 were waited for; matrix products, arithmetic and copies ran while one was open for 3% of the time, Pallas kernels for 11%

profile of v4, /device:TPU:0, one launch (start us, length us, event | category | flops | bytes accessed | tf_op | source)
XLA Modules:
  0.0 48.2 jit_solution(16193130795771123614)
XLA Ops:
  0.6 3.6 %shard_map.59 = (f32[256,128]{1,0:T(8,128)}, f32[5,32,128]{2,1,0:T(8,128)}, f32[5,32,128]{2,1,0:T(8,128)}, s32[64]{0:T(128)}, s32[18]{0:T(128)}) custom-call(s32[128]{0:T(128)} %box_ref.1, f32[5,8,32,128]{3,2,1,0:T(8,128)} %coarse_hbm.1), custom_call_target="tpu_custom_call" | custom-call | flops 1000000 | bytes 1000000 | tf_op jit(solution)/shard_map/pallas_call | solution.py:710
  4.3 7.5 %all-to-all-start = ((f32[16,16,128]{2,1,0:T(8,128)}), f32[16,16,128]{2,1,0:T(8,128)S(1)}, u32[]{:S(2)}, u32[]{:S(2)}) async-start(f32[16,16,128]{2,1,0:T(8,128)} %bitcast.15), calls=%async_computation | async-start | bytes 262144 | tf_op jit(solution)/shard_map/all_to_all | solution.py:731
  11.8 0.0 copy-start.1
  11.8 1.1 %copy-done.1 = f32[8,5,16,256]{3,2,1,0:T(8,128)S(1)} copy-done((f32[8,5,16,256]{3,2,1,0:T(8,128)S(1)}, f32[8,5,16,256]{3,2,1,0:T(8,128)}, u32[]{:S(2)}) %copy-start.1) | copy-done | bytes 655384
  12.9 2.5 %shard_map.60 = (f32[5,17,2,8,128]{4,3,2,1,0:T(8,128)S(1)}, f32[9,16,2,8,128]{4,3,2,1,0:T(8,128)S(1)}) custom-call(f32[8,5,16,256]{3,2,1,0:T(8,128)S(1)} %copy-done.1), custom_call_target="tpu_custom_call" | custom-call | flops 10000000 | bytes 4000000 | tf_op jit(solution)/shard_map/pallas_call | solution.py:735
  15.4 4.3 %all-to-all-done = f32[16,16,128]{2,1,0:T(8,128)S(1)} async-done(((f32[16,16,128]{2,1,0:T(8,128)}), f32[16,16,128]{2,1,0:T(8,128)S(1)}, u32[]{:S(2)}, u32[]{:S(2)}) %all-to-all-start) | async-done | bytes 131104 | tf_op jit(solution)/shard_map/all_to_all | solution.py:731
  19.7 0.0 copy-start.3
  19.7 0.7 %copy-done.3 = s32[128]{0:T(128)S(1)} copy-done((s32[128]{0:T(128)S(1)}, s32[128]{0:T(128)}, u32[]{:S(2)}) %copy-start.3) | copy-done | bytes 536
  20.4 0.0 copy-start
  20.4 4.8 %shard_map.61 = (f32[640,128]{1,0:T(8,128)S(1)}, f32[5,17,2,8,128]{4,3,2,1,0:T(8,128)S(1)}) custom-call(s32[128]{0:T(128)S(1)} %copy-done.3, f32[256,128]{1,0:T(8,128)S(1)} %bitcast.10, f32[5,17,2,8,128]{4,3,2,1,0:T(8,128)S(1)} %get-tuple-element.16.middle_ref, f32[9,16,2,8,128]{4,3,2,1,0:T(8,128)S(1)} %get-tuple-element.17.cells_ref), custom_call_target="tpu_custom_call" | custom-call | flops 20000000 | bytes 4000000 | tf_op jit(solution)/shard_map/pallas_call | solution.py:751
  25.2 0.0 copy-start.2
  25.2 0.7 %copy-done.2 = f32[640,128]{1,0:T(8,128)} copy-done((f32[640,128]{1,0:T(8,128)}, f32[640,128]{1,0:T(8,128)S(1)}, u32[]{:S(2)}) %copy-start.2) | copy-done | bytes 327704
  25.9 3.5 %all-to-all-start.1 = ((f32[16,40,128]{2,1,0:T(8,128)}), f32[16,40,128]{2,1,0:T(8,128)S(1)}, u32[]{:S(2)}, u32[]{:S(2)}) async-start(f32[16,40,128]{2,1,0:T(8,128)} %bitcast.11), calls=%async_computation.1 | async-start | bytes 655360 | tf_op jit(solution)/shard_map/all_to_all | solution.py:773
  29.5 0.3 collective-permute-start
  29.8 4.2 %collective-permute-start.1 = (f32[5,32,128]{2,1,0:T(8,128)}, f32[5,32,128]{2,1,0:T(8,128)S(1)}, u32[]{:S(2)}, u32[]{:S(2)}) collective-permute-start(f32[5,32,128]{2,1,0:T(8,128)} %get-tuple-element.20), channel_id=1, source_target_pairs={{1,0},{2,1},{3,2},{4,3},{5,4},{6,5},{7,6},{8,7},{9,8},{10,9},{11,1... | collective-permute-start | bytes 245768 | tf_op jit(solution)/shard_map/ppermute | solution.py:734
  34.0 0.8 %copy.6 = s32[128,6]{1,0:T(8,128)S(1)} copy(s32[128,6]{0,1:T(8,128)} %param.7) | data formatting | bytes 6144 | tf_op args[3]
  34.8 0.1 reshape.31
  34.9 0.8 %pad_add_fusion.slot_ref = s32[960]{0:T(1024)S(1)} fusion(s32[768]{0:T(1024)S(1)} %reshape.31, s32[128]{0:T(128)} %box_ref.1, s32[64]{0:T(128)} %get-tuple-element.14), kind=kLoop, calls=%fused_computation | loop fusion | flops 1920 | bytes 7680 | tf_op jit(solution)/shard_map/concatenate | solution.py:783
  35.7 5.7 %collective-permute-done = f32[5,32,128]{2,1,0:T(8,128)S(1)} collective-permute-done((f32[5,32,128]{2,1,0:T(8,128)}, f32[5,32,128]{2,1,0:T(8,128)S(1)}, u32[]{:S(2)}, u32[]{:S(2)}) %collective-permute-start) | collective-permute-done | bytes 81952 | tf_op jit(solution)/shard_map/ppermute | solution.py:733
  41.4 0.0 collective-permute-done.1
  41.4 0.0 copy-done
  41.4 1.9 %shard_map.62 = (f32[1280,128]{1,0:T(8,128)S(1)}, f32[1280,128]{1,0:T(8,128)S(1)}, f32[160,128]{1,0:T(8,128)S(1)}, f32[320,128]{1,0:T(8,128)S(1)}) custom-call(f32[1280,128]{1,0:T(8,128)S(1)} %bitcast.8, f32[160,128]{1,0:T(8,128)S(1)} %bitcast.12, f32[160,128]{1,0:T(8,128)S(1)} %bitcast.13), custom_call_target="tpu_custom_call" | custom-call | flops 10000000 | bytes 4000000 | tf_op jit(solution)/shard_map/pallas_call | solution.py:785
  43.3 1.0 %shard_map.64 = f32[8,5,16,256]{3,2,1,0:T(8,128)} custom-call(f32[5,17,2,8,128]{4,3,2,1,0:T(8,128)S(1)} %get-tuple-element.25.state_ref), custom_call_target="tpu_custom_call" | custom-call | flops 1000000 | bytes 4000000 | tf_op jit(solution)/shard_map/pallas_call | solution.py:774
  44.3 0.0 all-to-all-done.1
  44.3 3.9 %shard_map.63 = f32[1280,128]{1,0:T(8,128)} custom-call(s32[960]{0:T(1024)S(1)} %pad_add_fusion.slot_ref, f32[640,128]{1,0:T(8,128)S(1)} %bitcast.9, f32[1280,128]{1,0:T(8,128)S(1)} %get-tuple-element.21.base_ref, f32[1280,128]{1,0:T(8,128)S(1)} %get-tuple-element.22.yedge_ref, f32[160,128]{1,0:T(8,128)S(1)} %get-tuple-element.23.zedge_ref, ...), custom_call_target="tpu_custom_call" | custom-call | flops 2000000 | bytes 4000000 | tf_op jit(solution)/shard_map/pallas_call | solution.py:794
Async XLA Ops:
  4.3 15.4 %all-to-all-start = ((f32[16,16,128]{2,1,0:T(8,128)}), f32[16,16,128]{2,1,0:T(8,128)S(1)}, u32[]{:S(2)}, u32[]{:S(2)}) async-start(f32[16,16,128]{2,1,0:T(8,128)} %bitcast.15), calls=%async_computation | async-start | bytes 262144 | tf_op jit(solution)/shard_map/all_to_all | solution.py:731
  11.8 1.1 %copy-start.1 = (f32[8,5,16,256]{3,2,1,0:T(8,128)S(1)}, f32[8,5,16,256]{3,2,1,0:T(8,128)}, u32[]{:S(2)}) copy-start(f32[8,5,16,256]{3,2,1,0:T(8,128)} %fine_ref.1) | copy-start | bytes 1966084
  19.7 0.7 %copy-start.3 = (s32[128]{0:T(128)S(1)}, s32[128]{0:T(128)}, u32[]{:S(2)}) copy-start(s32[128]{0:T(128)} %box_ref.1) | copy-start | bytes 1540
  20.4 21.1 %copy-start = (f32[5,8,32,128]{3,2,1,0:T(8,128)S(1)}, f32[5,8,32,128]{3,2,1,0:T(8,128)}, u32[]{:S(2)}) copy-start(f32[5,8,32,128]{3,2,1,0:T(8,128)} %coarse_hbm.1) | copy-start | bytes 1966084
  25.2 0.7 %copy-start.2 = (f32[640,128]{1,0:T(8,128)}, f32[640,128]{1,0:T(8,128)S(1)}, u32[]{:S(2)}) copy-start(f32[640,128]{1,0:T(8,128)S(1)} %get-tuple-element.18) | copy-start | bytes 983044
  25.9 18.4 %all-to-all-start.1 = ((f32[16,40,128]{2,1,0:T(8,128)}), f32[16,40,128]{2,1,0:T(8,128)S(1)}, u32[]{:S(2)}, u32[]{:S(2)}) async-start(f32[16,40,128]{2,1,0:T(8,128)} %bitcast.11), calls=%async_computation.1 | async-start | bytes 655360 | tf_op jit(solution)/shard_map/all_to_all | solution.py:773
  29.5 11.9 %collective-permute-start = (f32[5,32,128]{2,1,0:T(8,128)}, f32[5,32,128]{2,1,0:T(8,128)S(1)}, u32[]{:S(2)}, u32[]{:S(2)}) collective-permute-start(f32[5,32,128]{2,1,0:T(8,128)} %get-tuple-element.19), channel_id=1, source_target_pairs={{0,1},{1,2},{2,3},{3,4},{4,5},{5,6},{6,7},{7,8},{8,9},{9,10},{10,1... | collective-permute-start | bytes 245768 | tf_op jit(solution)/shard_map/ppermute | solution.py:733
  29.8 11.6 %collective-permute-start.1 = (f32[5,32,128]{2,1,0:T(8,128)}, f32[5,32,128]{2,1,0:T(8,128)S(1)}, u32[]{:S(2)}, u32[]{:S(2)}) collective-permute-start(f32[5,32,128]{2,1,0:T(8,128)} %get-tuple-element.20), channel_id=1, source_target_pairs={{1,0},{2,1},{3,2},{4,3},{5,4},{6,5},{7,6},{8,7},{9,8},{10,9},{11,1... | collective-permute-start | bytes 245768 | tf_op jit(solution)/shard_map/ppermute | solution.py:734

commit v5 on v4

--- a/solution.py
+++ b/solution.py
@@ -57,6 +57,16 @@
 def face_flux(left, right):
     fastest = jnp.maximum(left[10], right[10])
     return [left[5 + f] + right[5 + f] - fastest * (right[f] - left[f]) for f in range(NF)]
+
+
+def raw_of(cells, prims, m):
+    return cells + [prims[0][m], prims[1], prims[2]]
+
+
+def side_of_raw(raw, m):
+    speeds = [None] * 4
+    speeds[m] = raw[5]
+    return side_of_face(raw[:NF], (speeds, raw[6], raw[7], raw[4] + raw[6]), m)
 
 
 def split_box(number, per_device):
@@ -230,9 +240,11 @@
                     carry[i, c] = here[i]
                 for f in range(NF):
                     middle_ref[f, x, c] = carry[11 + f, c] - step * flux[f]
-            here = [side_of_face(cells[c], prims[c], 3) for c in range(2)]
-            turned = [[roll_to(v, 16) for v in here[c]] for c in range(2)]
-            left = [turned[0], [jnp.where(low16, turned[0][i], turned[1][i]) for i in range(11)]]
+            raw = [raw_of(cells[c], prims[c], 3) for c in range(2)]
+            here = [side_of_raw(raw[c], 3) for c in range(2)]
+            turned = [[roll_to(v, 16) for v in raw[c]] for c in range(2)]
+            left = [turned[0], [jnp.where(low16, a, b) for a, b in zip(*turned)]]
+            left = [side_of_raw(v, 3) for v in left]
             lower = [face_flux(left[c], here[c]) for c in range(2)]
             lower[0] = [jnp.where(low16, 0.0, v) for v in lower[0]]
             change = [[], []]
@@ -241,8 +253,9 @@
                 change[0].append(jnp.where(high16, back[0], back[1]) - lower[0][f])
                 change[1].append(jnp.where(high16, back[1], back[0]) - lower[1][f])
             for c in range(2):
-                here = side_of_face(cells[c], prims[c], 2)
-                lower_y = face_flux([roll_to(v, 1) for v in here], here)
+                raw = raw_of(cells[c], prims[c], 2)
+                here = side_of_raw(raw, 2)
+                lower_y = face_flux(side_of_raw([roll_to(v, 1) for v in raw], 2), here)
                 lower_y = [jnp.where(first_y, 0.0, v) for v in lower_y]
                 for f in range(NF):
                     total = change[c][f] + (roll_to(lower_y[f], -1) - lower_y[f]) - flux_x[c][f]
@@ -394,14 +407,6 @@
         for f in range(NF):
             xsum[side, f] = flux_x[f]
             middle[f, plane] = middle[f, plane] + (-step if side else step) * flux_x[f]
-
-    def raw_of(cells, prims, m):
-        return cells + [prims[0][m], prims[1], prims[2]]
-
-    def side_of_raw(raw, m):
-        speeds = [None] * 4
-        speeds[m] = raw[5]
-        return side_of_face(raw[:NF], (speeds, raw[6], raw[7], raw[4] + raw[6]), m)
 
     def finish(plane, part, flux):
         for c in range(2):

time: 48.7 us -> 48.7 us (level)
  no operation moved by 1% of the time
where the time goes in v5:
time: 48.7 us; the launch traced here: 48.2 us
  Pallas kernels  17.8 us (37%)
  starting transfers between devices  15.6 us (32%)
  waiting for transfers between devices  10 us (21%)
  local copies, waits for them, and re-layouts  3.38 us (7%)
  other arithmetic  0.76 us (2%)
  between operations  0.72 us (1%)
    all_to_all x1, starting transfers between devices, local(): lax.all_to_all(packets.reshape(count, 16, LN), 'box', split_axis=0, conca...  7.54 us
    ppermute x1, waiting for transfers between devices, local(): low = lax.ppermute(last, 'box', ring)  5.72 us
    pallas_call x1, Pallas kernels, local(): call(functools.partial(fine_kernel, count), (shaped(count * 40, LN), shap...  4.85 us
    all_to_all x1, waiting for transfers between devices, local(): lax.all_to_all(packets.reshape(count, 16, LN), 'box', split_axis=0, conca...  4.32 us
    ppermute x1, starting transfers between devices, local(): high = lax.ppermute(first, 'box', [(b, a) for a, b in ring])  4.2 us
    pallas_call x1, Pallas kernels, local(): call(functools.partial(apply_kernel, count), shaped(size, LN), [smem] + [...  3.93 us
    pallas_call x1, Pallas kernels, local(): call(functools.partial(pack_kernel, count), (shaped(count * 16, LN), shap...  3.62 us
    all_to_all x1, starting transfers between devices, local(): lax.all_to_all(outbox.reshape(count, 40, LN), 'box', split_axis=0, concat...  3.54 us
  transfers between devices with their start and end apart: 4, of which 2 were waited for; matrix products, arithmetic and copies ran while one was open for 3% of the time, Pallas kernels for 11%

profile of v5, /device:TPU:0, one launch (start us, length us, event | category | flops | bytes accessed | tf_op | source)
XLA Modules:
  0.0 48.2 jit_solution(308190718735939763)
XLA Ops:
  0.6 3.6 %shard_map.59 = (f32[256,128]{1,0:T(8,128)}, f32[5,32,128]{2,1,0:T(8,128)}, f32[5,32,128]{2,1,0:T(8,128)}, s32[64]{0:T(128)}, s32[18]{0:T(128)}) custom-call(s32[128]{0:T(128)} %box_ref.1, f32[5,8,32,128]{3,2,1,0:T(8,128)} %coarse_hbm.1), custom_call_target="tpu_custom_call" | custom-call | flops 1000000 | bytes 1000000 | tf_op jit(solution)/shard_map/pallas_call | solution.py:715
  4.3 7.5 %all-to-all-start = ((f32[16,16,128]{2,1,0:T(8,128)}), f32[16,16,128]{2,1,0:T(8,128)S(1)}, u32[]{:S(2)}, u32[]{:S(2)}) async-start(f32[16,16,128]{2,1,0:T(8,128)} %bitcast.15), calls=%async_computation | async-start | bytes 262144 | tf_op jit(solution)/shard_map/all_to_all | solution.py:736
  11.8 0.0 copy-start.1
  11.8 1.1 %copy-done.1 = f32[8,5,16,256]{3,2,1,0:T(8,128)S(1)} copy-done((f32[8,5,16,256]{3,2,1,0:T(8,128)S(1)}, f32[8,5,16,256]{3,2,1,0:T(8,128)}, u32[]{:S(2)}) %copy-start.1) | copy-done | bytes 655384
  12.9 2.5 %shard_map.60 = (f32[5,17,2,8,128]{4,3,2,1,0:T(8,128)S(1)}, f32[9,16,2,8,128]{4,3,2,1,0:T(8,128)S(1)}) custom-call(f32[8,5,16,256]{3,2,1,0:T(8,128)S(1)} %copy-done.1), custom_call_target="tpu_custom_call" | custom-call | flops 10000000 | bytes 4000000 | tf_op jit(solution)/shard_map/pallas_call | solution.py:740
  15.4 4.3 %all-to-all-done = f32[16,16,128]{2,1,0:T(8,128)S(1)} async-done(((f32[16,16,128]{2,1,0:T(8,128)}), f32[16,16,128]{2,1,0:T(8,128)S(1)}, u32[]{:S(2)}, u32[]{:S(2)}) %all-to-all-start) | async-done | bytes 131104 | tf_op jit(solution)/shard_map/all_to_all | solution.py:736
  19.7 0.0 copy-start.3
  19.7 0.7 %copy-done.3 = s32[128]{0:T(128)S(1)} copy-done((s32[128]{0:T(128)S(1)}, s32[128]{0:T(128)}, u32[]{:S(2)}) %copy-start.3) | copy-done | bytes 536
  20.4 0.0 copy-start
  20.4 4.8 %shard_map.61 = (f32[640,128]{1,0:T(8,128)S(1)}, f32[5,17,2,8,128]{4,3,2,1,0:T(8,128)S(1)}) custom-call(s32[128]{0:T(128)S(1)} %copy-done.3, f32[256,128]{1,0:T(8,128)S(1)} %bitcast.10, f32[5,17,2,8,128]{4,3,2,1,0:T(8,128)S(1)} %get-tuple-element.16.middle_ref, f32[9,16,2,8,128]{4,3,2,1,0:T(8,128)S(1)} %get-tuple-element.17.cells_ref), custom_call_target="tpu_custom_call" | custom-call | flops 20000000 | bytes 4000000 | tf_op jit(solution)/shard_map/pallas_call | solution.py:756
  25.2 0.0 copy-start.2
  25.2 0.7 %copy-done.2 = f32[640,128]{1,0:T(8,128)} copy-done((f32[640,128]{1,0:T(8,128)}, f32[640,128]{1,0:T(8,128)S(1)}, u32[]{:S(2)}) %copy-start.2) | copy-done | bytes 327704
  25.9 3.5 %all-to-all-start.1 = ((f32[16,40,128]{2,1,0:T(8,128)}), f32[16,40,128]{2,1,0:T(8,128)S(1)}, u32[]{:S(2)}, u32[]{:S(2)}) async-start(f32[16,40,128]{2,1,0:T(8,128)} %bitcast.11), calls=%async_computation.1 | async-start | bytes 655360 | tf_op jit(solution)/shard_map/all_to_all | solution.py:778
  29.5 0.3 collective-permute-start
  29.8 4.2 %collective-permute-start.1 = (f32[5,32,128]{2,1,0:T(8,128)}, f32[5,32,128]{2,1,0:T(8,128)S(1)}, u32[]{:S(2)}, u32[]{:S(2)}) collective-permute-start(f32[5,32,128]{2,1,0:T(8,128)} %get-tuple-element.20), channel_id=1, source_target_pairs={{1,0},{2,1},{3,2},{4,3},{5,4},{6,5},{7,6},{8,7},{9,8},{10,9},{11,1... | collective-permute-start | bytes 245768 | tf_op jit(solution)/shard_map/ppermute | solution.py:739
  34.0 0.8 %copy.6 = s32[128,6]{1,0:T(8,128)S(1)} copy(s32[128,6]{0,1:T(8,128)} %param.7) | data formatting | bytes 6144 | tf_op args[3]
  34.8 0.1 reshape.31
  34.9 0.8 %pad_add_fusion.slot_ref = s32[960]{0:T(1024)S(1)} fusion(s32[768]{0:T(1024)S(1)} %reshape.31, s32[128]{0:T(128)} %box_ref.1, s32[64]{0:T(128)} %get-tuple-element.14), kind=kLoop, calls=%fused_computation | loop fusion | flops 1920 | bytes 7680 | tf_op jit(solution)/shard_map/concatenate | solution.py:788
  35.7 5.7 %collective-permute-done = f32[5,32,128]{2,1,0:T(8,128)S(1)} collective-permute-done((f32[5,32,128]{2,1,0:T(8,128)}, f32[5,32,128]{2,1,0:T(8,128)S(1)}, u32[]{:S(2)}, u32[]{:S(2)}) %collective-permute-start) | collective-permute-done | bytes 81952 | tf_op jit(solution)/shard_map/ppermute | solution.py:738
  41.4 0.0 collective-permute-done.1
  41.4 0.0 copy-done
  41.4 1.9 %shard_map.62 = (f32[1280,128]{1,0:T(8,128)S(1)}, f32[1280,128]{1,0:T(8,128)S(1)}, f32[160,128]{1,0:T(8,128)S(1)}, f32[320,128]{1,0:T(8,128)S(1)}) custom-call(f32[1280,128]{1,0:T(8,128)S(1)} %bitcast.8, f32[160,128]{1,0:T(8,128)S(1)} %bitcast.12, f32[160,128]{1,0:T(8,128)S(1)} %bitcast.13), custom_call_target="tpu_custom_call" | custom-call | flops 10000000 | bytes 4000000 | tf_op jit(solution)/shard_map/pallas_call | solution.py:790
  43.3 1.0 %shard_map.64 = f32[8,5,16,256]{3,2,1,0:T(8,128)} custom-call(f32[5,17,2,8,128]{4,3,2,1,0:T(8,128)S(1)} %get-tuple-element.25.state_ref), custom_call_target="tpu_custom_call" | custom-call | flops 1000000 | bytes 4000000 | tf_op jit(solution)/shard_map/pallas_call | solution.py:779
  44.3 0.0 all-to-all-done.1
  44.3 3.9 %shard_map.63 = f32[1280,128]{1,0:T(8,128)} custom-call(s32[960]{0:T(1024)S(1)} %pad_add_fusion.slot_ref, f32[640,128]{1,0:T(8,128)S(1)} %bitcast.9, f32[1280,128]{1,0:T(8,128)S(1)} %get-tuple-element.21.base_ref, f32[1280,128]{1,0:T(8,128)S(1)} %get-tuple-element.22.yedge_ref, f32[160,128]{1,0:T(8,128)S(1)} %get-tuple-element.23.zedge_ref, ...), custom_call_target="tpu_custom_call" | custom-call | flops 2000000 | bytes 4000000 | tf_op jit(solution)/shard_map/pallas_call | solution.py:799
Async XLA Ops:
  4.3 15.4 %all-to-all-start = ((f32[16,16,128]{2,1,0:T(8,128)}), f32[16,16,128]{2,1,0:T(8,128)S(1)}, u32[]{:S(2)}, u32[]{:S(2)}) async-start(f32[16,16,128]{2,1,0:T(8,128)} %bitcast.15), calls=%async_computation | async-start | bytes 262144 | tf_op jit(solution)/shard_map/all_to_all | solution.py:736
  11.8 1.1 %copy-start.1 = (f32[8,5,16,256]{3,2,1,0:T(8,128)S(1)}, f32[8,5,16,256]{3,2,1,0:T(8,128)}, u32[]{:S(2)}) copy-start(f32[8,5,16,256]{3,2,1,0:T(8,128)} %fine_ref.1) | copy-start | bytes 1966084
  19.7 0.7 %copy-start.3 = (s32[128]{0:T(128)S(1)}, s32[128]{0:T(128)}, u32[]{:S(2)}) copy-start(s32[128]{0:T(128)} %box_ref.1) | copy-start | bytes 1540
  20.4 21.1 %copy-start = (f32[5,8,32,128]{3,2,1,0:T(8,128)S(1)}, f32[5,8,32,128]{3,2,1,0:T(8,128)}, u32[]{:S(2)}) copy-start(f32[5,8,32,128]{3,2,1,0:T(8,128)} %coarse_hbm.1) | copy-start | bytes 1966084
  25.2 0.7 %copy-start.2 = (f32[640,128]{1,0:T(8,128)}, f32[640,128]{1,0:T(8,128)S(1)}, u32[]{:S(2)}) copy-start(f32[640,128]{1,0:T(8,128)S(1)} %get-tuple-element.18) | copy-start | bytes 983044
  25.9 18.4 %all-to-all-start.1 = ((f32[16,40,128]{2,1,0:T(8,128)}), f32[16,40,128]{2,1,0:T(8,128)S(1)}, u32[]{:S(2)}, u32[]{:S(2)}) async-start(f32[16,40,128]{2,1,0:T(8,128)} %bitcast.11), calls=%async_computation.1 | async-start | bytes 655360 | tf_op jit(solution)/shard_map/all_to_all | solution.py:778
  29.5 11.9 %collective-permute-start = (f32[5,32,128]{2,1,0:T(8,128)}, f32[5,32,128]{2,1,0:T(8,128)S(1)}, u32[]{:S(2)}, u32[]{:S(2)}) collective-permute-start(f32[5,32,128]{2,1,0:T(8,128)} %get-tuple-element.19), channel_id=1, source_target_pairs={{0,1},{1,2},{2,3},{3,4},{4,5},{5,6},{6,7},{7,8},{8,9},{9,10},{10,1... | collective-permute-start | bytes 245768 | tf_op jit(solution)/shard_map/ppermute | solution.py:738
  29.8 11.6 %collective-permute-start.1 = (f32[5,32,128]{2,1,0:T(8,128)}, f32[5,32,128]{2,1,0:T(8,128)S(1)}, u32[]{:S(2)}, u32[]{:S(2)}) collective-permute-start(f32[5,32,128]{2,1,0:T(8,128)} %get-tuple-element.20), channel_id=1, source_target_pairs={{1,0},{2,1},{3,2},{4,3},{5,4},{6,5},{7,6},{8,7},{9,8},{10,9},{11,1... | collective-permute-start | bytes 245768 | tf_op jit(solution)/shard_map/ppermute | solution.py:739
